TPU v7x, 32 devices: a whole 2x2x4 slice. The times are simulated.
32 devices in a mesh: pipe: 4 (over y, core), expert: 2 (over x), dp: 4 (over z).
Axes of the slice: x: 2, y: 2, z: 4, core: 2. Of those that a mesh axis runs over, the one named last changes fastest.
Arguments:
- tokens: bfloat16 [4, 1024, 3072], P('pipe', ('expert', 'dp')), may hold values from -6 to 6
- grad_out: bfloat16 [4, 1024, 3072], P('pipe', ('expert', 'dp')), may hold values from -6 to 6
- routes: int32 [4, 1024, 2], P('pipe', ('expert', 'dp')), may hold values from 0 to 7, as said below
- route_weights: float32 [4, 1024, 2], P('pipe', ('expert', 'dp')), may hold values from 0.1 to 0.9
- gate_weight: bfloat16 [4, 3072, 32768], P('pipe', None, ('expert', 'dp')), may hold values from -0.109375 to 0.109375
- up_weight: bfloat16 [4, 3072, 32768], P('pipe', None, ('expert', 'dp')), may hold values from -0.109375 to 0.109375
- down_weight: bfloat16 [4, 32768, 3072], P('pipe', ('expert', 'dp')), may hold values from -0.046875 to 0.046875
Outputs:
- upstream: bfloat16 [4, 1024, 3072], P('pipe', ('expert', 'dp'))
Inputs may be any that keep to these rules, and one draw needn't show every extreme that they name: `routes`: each row names two different experts. In every section, for each window expert e < 2, the tokens of one device that name e number 1 to 8, exactly 8 on some device, and the tokens of the whole section name e exactly 36 times.
All inputs are finite; a program needn't handle non-finite values.
Results may differ from a plain program's by a relative error of at most 0.0013.
Values may be sent and summed in bfloat16 or wider, within the bound.
No kernel may reach another device: no remote copies, remote signals or barrier semaphores. Data moves between devices by JAX's collectives and lax.ppermute only.
A program may use at most 192 MiB of HBM per device.

v0:
```python
import jax
import jax.numpy as jnp
from jax import lax
from jax.sharding import PartitionSpec as P

EF = 2
CAP = 8


def from_behind(value, axis, steps):
    count = lax.axis_size(axis)
    first, last = (max(0, -steps), min(count, count - steps))
    return lax.ppermute(value, axis, [(source, source + steps) for source in range(first, last)])


def hidden_grads(rows_in, rows_grad, gate_slice, up_slice, down_slice):
    gate_pre = jnp.dot(rows_in, gate_slice, preferred_element_type=jnp.float32)
    up_pre = jnp.dot(rows_in, up_slice, preferred_element_type=jnp.float32)
    sigmoid_gate = jax.nn.sigmoid(gate_pre)
    contract = (((1,), (1,)), ((), ()))
    act_grad = lax.dot_general(rows_grad, down_slice, contract, preferred_element_type=jnp.float32)
    gate_grad = (act_grad * up_pre * sigmoid_gate * (1.0 + gate_pre * (1.0 - sigmoid_gate))).astype(
        jnp.bfloat16
    )
    up_grad = (act_grad * gate_pre * sigmoid_gate).astype(jnp.bfloat16)
    result = lax.dot_general(gate_grad, gate_slice, contract, preferred_element_type=jnp.float32)
    return result + lax.dot_general(up_grad, up_slice, contract, preferred_element_type=jnp.float32)


def shards(tokens, grad_out, routes, route_weights, gate_weight, up_weight, down_weight):
    expert_count = lax.axis_size("expert")
    data_count = lax.axis_size("dp")
    device_count = expert_count * data_count
    group_size = device_count // EF
    inputs = tokens[0]
    upstream_grad = grad_out[0]
    picks = routes[0]
    pick_weights = route_weights[0]
    width = inputs.shape[1]
    capacity = CAP
    slot_range = jnp.arange(capacity, dtype=jnp.int32)
    upstream_float = upstream_grad.astype(jnp.float32)
    sent_inputs = []
    sent_grads = []
    sent_counts = []
    chosen_sets = []
    slot_places = []
    for expert in range(EF):
        first_pick = picks[:, 0] == expert
        second_pick = picks[:, 1] == expert
        chosen = first_pick | second_pick
        weight = jnp.where(first_pick, pick_weights[:, 0], 0.0) + jnp.where(
            second_pick, pick_weights[:, 1], 0.0
        )
        slot_place = jnp.cumsum(chosen.astype(jnp.int32)) - 1
        slot_table = ((slot_place[None, :] == slot_range[:, None]) & chosen[None, :]).astype(
            jnp.bfloat16
        )
        scaled = (weight[:, None] * upstream_float).astype(jnp.bfloat16)
        sent_inputs.append(
            jnp.dot(slot_table, inputs, preferred_element_type=jnp.float32).astype(jnp.bfloat16)
        )
        sent_grads.append(
            jnp.dot(slot_table, scaled, preferred_element_type=jnp.float32).astype(jnp.bfloat16)
        )
        sent_counts.append(jnp.sum(chosen.astype(jnp.int32)))
        chosen_sets.append(chosen)
        slot_places.append(jnp.clip(slot_place, 0, capacity - 1))
    stack_inputs = jnp.stack(sent_inputs)
    stack_grads = jnp.stack(sent_grads)
    stack_counts = jnp.stack(sent_counts)
    bound_inputs = jnp.repeat(stack_inputs, group_size, axis=0)
    bound_grads = jnp.repeat(stack_grads, group_size, axis=0)
    bound_counts = jnp.repeat(stack_counts, group_size)[:, None]
    recv_inputs, recv_grads, recv_counts = (
        lax.all_to_all(bound_inputs, ("expert", "dp"), split_axis=0, concat_axis=0, tiled=True),
        lax.all_to_all(bound_grads, ("expert", "dp"), split_axis=0, concat_axis=0, tiled=True),
        lax.all_to_all(bound_counts, ("expert", "dp"), split_axis=0, concat_axis=0, tiled=True),
    )
    rows_in = recv_inputs.reshape(device_count * capacity, width)
    rows_grad = recv_grads.reshape(device_count * capacity, width)
    counts_in = recv_counts[:, 0]
    live_slots = (slot_range[None, :] < counts_in[:, None]).reshape(-1)
    gate_slice = gate_weight[0]
    up_slice = up_weight[0]
    down_slice = down_weight[0]
    partial_value = hidden_grads(rows_in, rows_grad, gate_slice, up_slice, down_slice) * live_slots[
        :, None
    ].astype(jnp.float32)
    partial_bf = partial_value.astype(jnp.bfloat16).reshape(device_count, capacity, width)
    returned = lax.all_to_all(partial_bf, ("expert", "dp"), split_axis=0, concat_axis=0, tiled=True)
    summed = returned.astype(jnp.float32).reshape(EF, group_size, capacity, width).sum(axis=1)
    branch = jnp.zeros_like(upstream_float)
    for expert in range(EF):
        picked_rows = summed[expert][slot_places[expert]]
        branch = branch + jnp.where(chosen_sets[expert][:, None], picked_rows, 0.0)
    grad_in = (upstream_float + branch).astype(jnp.bfloat16)[None]
    return from_behind(grad_in, "pipe", -1)


def solution(mesh):
    placed = (
        P("pipe", ("expert", "dp"), None),
        P("pipe", ("expert", "dp"), None),
        P("pipe", ("expert", "dp"), None),
        P("pipe", ("expert", "dp"), None),
        P("pipe", None, ("expert", "dp")),
        P("pipe", None, ("expert", "dp")),
        P("pipe", ("expert", "dp"), None),
    )
    return jax.shard_map(
        shards,
        mesh=mesh,
        in_specs=placed,
        out_specs=P("pipe", ("expert", "dp"), None),
        check_vma=False,
    )
```

profile of v0, /device:TPU:1, one launch (start us, length us, event | category | flops | bytes accessed | tf_op | source)
XLA Modules:
  0.0 130.9 jit_solution(7416122396753780305)
XLA Ops:
  0.0 0.9 copy.15
  1.1 0.7 convert_reduce_fusion.1
  1.8 1.4 %pad_add_fusion = s32[2]{0:T(128)S(1)} fusion(s32[1]{0:T(128)} %bitcast.16, s32[1]{0:T(128)} %bitcast.15), kind=kLoop, calls=%fused_computation.89 | loop fusion | flops 2 | bytes 16 | tf_op jit(solution)/shard_map/stack | solution.py:71
  4.0 6.4 %all-to-all-start.2 = ((s32[8,1,1]{2,1,0:T(1,128)}), s32[8,1,1]{2,1,0:T(1,128)S(1)}, u32[]{:S(2)}, u32[]{:S(2)}) async-start(s32[8,1,1]{2,1,0:T(1,128)} %all_to_all.20), calls=%async_computation.2 | async-start | bytes 8192 | tf_op jit(solution)/shard_map/all_to_all | solution.py:78
  10.3 0.8 copy.16
  11.9 1.4 %fusion.44 = bf16[1,8,3072]{2,1,0:T(8,128)(2,1)S(1)} fusion(bf16[1,128,3072]{2,1,0:T(8,128)(2,1)} %param.8, f32[128]{0:T(128)S(1)} %get-tuple-element.9, s32[128]{0:T(128)S(1)} %get-tuple-element.6, pred[128]{0:T(512)(128)(4,1)S(1)} %get-tuple-element.19), kind=kOutput, calls=%fused_computation.24 | convolution fusion | flops 7497728 | bytes 836736 | tf_op jit(solution)/shard_map/dot_general | solution.py:64
  13.9 1.7 %all-to-all-done.2 = s32[8,1,1]{2,1,0:T(1,128)S(1)} async-done(((s32[8,1,1]{2,1,0:T(1,128)}), s32[8,1,1]{2,1,0:T(1,128)S(1)}, u32[]{:S(2)}, u32[]{:S(2)}) %all-to-all-start.2) | async-done | bytes 64 | tf_op jit(solution)/shard_map/all_to_all | solution.py:78
  15.6 0.8 broadcast_in_dim.53
  16.3 3.8 %all-to-all-start = ((bf16[8,8,3072]{2,1,0:T(8,128)(2,1)}), bf16[8,8,3072]{2,1,0:T(8,128)(2,1)S(1)}, u32[]{:S(2)}, u32[]{:S(2)}) async-start(bf16[8,8,3072]{2,1,0:T(8,128)(2,1)} %bitcast.5), calls=%async_computation | async-start | bytes 786432 | tf_op jit(solution)/shard_map/all_to_all | solution.py:77
  20.8 8.8 %all-to-all-done = bf16[8,8,3072]{2,1,0:T(8,128)(2,1)S(1)} async-done(((bf16[8,8,3072]{2,1,0:T(8,128)(2,1)}), bf16[8,8,3072]{2,1,0:T(8,128)(2,1)S(1)}, u32[]{:S(2)}, u32[]{:S(2)}) %all-to-all-start) | async-done | bytes 393248 | tf_op jit(solution)/shard_map/all_to_all | solution.py:77
  29.6 0.8 broadcast_in_dim.54
  30.4 5.2 %all-to-all-start.1 = ((bf16[8,8,3072]{2,1,0:T(8,128)(2,1)}), bf16[8,8,3072]{2,1,0:T(8,128)(2,1)S(1)}, u32[]{:S(2)}, u32[]{:S(2)}) async-start(bf16[8,8,3072]{2,1,0:T(8,128)(2,1)} %bitcast.11), calls=%async_computation.1 | async-start | bytes 786432 | tf_op jit(solution)/shard_map/all_to_all | solution.py:76
  35.6 12.4 %fusion.8 = f32[64,4096]{1,0:T(8,128)S(1)} fusion(bf16[1,4096,3072]{2,1,0:T(8,128)(2,1)} %param.13, bf16[8,8,3072]{2,1,0:T(8,128)(2,1)S(1)} %all-to-all-done), kind=kOutput, calls=%fused_computation.10 | convolution fusion | flops 1610612736 | bytes 26607616 | tf_op jit(solution)/shard_map/dot_general | solution.py:21
  48.1 10.5 %fusion.2 = f32[64,4096]{1,0:T(8,128)S(1)} fusion(bf16[1,3072,4096]{2,1,0:T(8,128)(2,1)} %param.11, bf16[8,8,3072]{2,1,0:T(8,128)(2,1)S(1)} %all-to-all-done.1), kind=kOutput, calls=%fused_computation.4 | convolution fusion | flops 1610612736 | bytes 26607616 | tf_op jit(solution)/shard_map/dot_general | solution.py:17
  58.5 13.3 %fusion.4 = f32[64,3072]{1,0:T(8,128)} fusion(bf16[1,3072,4096]{2,1,0:T(8,128)(2,1)} %param.12, f32[64,4096]{1,0:T(8,128)S(1)} %fusion.8, f32[64,4096]{1,0:T(8,128)S(1)} %fusion.2), kind=kOutput, calls=%fused_computation.6 | convolution fusion | flops 1612185600 | bytes 28049408 | tf_op jit(solution)/shard_map/dot_general | solution.py:27
  71.8 20.9 %fusion.39 = bf16[8,8,3072]{2,1,0:T(8,128)(2,1)} fusion(f32[64,3072]{1,0:T(8,128)} %fusion.4, bf16[1,3072,4096]{2,1,0:T(8,128)(2,1)} %param.11, f32[64,4096]{1,0:T(8,128)S(1)} %fusion.8, bf16[1,3072,4096]{2,1,0:T(8,128)(2,1)} %param.12, f32[64,4096]{1,0:T(8,128)S(1)} %fusion.2, bf16[8,8,3072]{2,1,0:T(8,128)(2,1)S(1)} %all-to-all-done.1, f32[64]{0:T(128)S(1)} %reshape.211), kind=kOutput, calls=%fused_computation.19 | convolution fusion | flops 3224436736 | bytes 54001920 | tf_op jit(solution)/shard_map/dot_general | solution.py:26
  92.8 5.4 %all-to-all-start.3 = ((bf16[8,8,3072]{2,1,0:T(8,128)(2,1)}), bf16[8,8,3072]{2,1,0:T(8,128)(2,1)S(1)}, u32[]{:S(2)}, u32[]{:S(2)}) async-start(bf16[8,8,3072]{2,1,0:T(8,128)(2,1)} %fusion.39), calls=%async_computation.3 | async-start | bytes 786432 | tf_op jit(solution)/shard_map/all_to_all | solution.py:91
  98.2 8.7 %all-to-all-done.3 = bf16[8,8,3072]{2,1,0:T(8,128)(2,1)S(1)} async-done(((bf16[8,8,3072]{2,1,0:T(8,128)(2,1)}), bf16[8,8,3072]{2,1,0:T(8,128)(2,1)S(1)}, u32[]{:S(2)}, u32[]{:S(2)}) %all-to-all-start.3) | async-done | bytes 393248 | tf_op jit(solution)/shard_map/all_to_all | solution.py:91
  107.0 1.2 gather_fusion
  108.2 2.3 %gather_fusion.1 = f32[128,3072]{1,0:T(8,128)} fusion(f32[8,3072]{1,0:T(8,128)S(1)} %get-tuple-element.18, s32[1024]{0:T(1024)S(1)} %pad_clamp_fusion), kind=kCustom, calls=%fused_computation.1 | custom fusion | bytes 3146240 | tf_op jit(solution)/shard_map/gather | solution.py:95
  110.5 1.9 %fusion.52 = bf16[1,128,3072]{2,1,0:T(8,128)(2,1)S(1)} fusion(bf16[1,128,3072]{2,1,0:T(8,128)(2,1)S(1)} %copy-done.3, f32[128,3072]{1,0:T(8,128)} %gather_fusion.1, f32[128,3072]{1,0:T(8,128)S(1)} %gather_fusion, pred[128]{0:T(512)(128)(4,1)S(1)} %get-tuple-element.14, pred[128]{0:T(512)(128)(4,1)S(1)} %get-tuple-element.19), kind=kLoop, calls=%fused_computation.34 | loop fusion | flops 2359296 | bytes 4718848 | tf_op jit(solution)/shard_map/convert_element_type | solution.py:97
  112.4 6.8 %collective-permute-start = (bf16[1,128,3072]{2,1,0:T(8,128)(2,1)S(1)}, bf16[1,128,3072]{2,1,0:T(8,128)(2,1)S(1)}, u32[]{:S(2)}, u32[]{:S(2)}) collective-permute-start(bf16[1,128,3072]{2,1,0:T(8,128)(2,1)S(1)} %fusion.52), channel_id=1, source_target_pairs={{8,0},{16,8},{24,16},{9,1},{17,9},{25,17},{10,2},{18,10},{26,18},{... | collective-permute-start | bytes 2359304 | tf_op jit(solution)/shard_map/ppermute | solution.py:13
  119.2 10.8 %collective-permute-done = bf16[1,128,3072]{2,1,0:T(8,128)(2,1)S(1)} collective-permute-done((bf16[1,128,3072]{2,1,0:T(8,128)(2,1)S(1)}, bf16[1,128,3072]{2,1,0:T(8,128)(2,1)S(1)}, u32[]{:S(2)}, u32[]{:S(2)}) %collective-permute-start) | collective-permute-done | bytes 786464 | tf_op jit(solution)/shard_map/ppermute | solution.py:13
  130.0 0.9 copy.19
  (30 shorter events, 3.0 us)
Async XLA Ops:
  0.0 13.7 %copy-start = (bf16[1,128,3072]{2,1,0:T(8,128)(2,1)S(1)}, bf16[1,128,3072]{2,1,0:T(8,128)(2,1)}, u32[]{:S(2)}) copy-start(bf16[1,128,3072]{2,1,0:T(8,128)(2,1)} %param.7) | copy-start | bytes 2359300
  0.0 13.3 %copy-start.2 = (bf16[1,128,3072]{2,1,0:T(8,128)(2,1)S(1)}, bf16[1,128,3072]{2,1,0:T(8,128)(2,1)}, u32[]{:S(2)}) copy-start(bf16[1,128,3072]{2,1,0:T(8,128)(2,1)} %param.8) | copy-start | bytes 2359300
  4.0 11.6 %all-to-all-start.2 = ((s32[8,1,1]{2,1,0:T(1,128)}), s32[8,1,1]{2,1,0:T(1,128)S(1)}, u32[]{:S(2)}, u32[]{:S(2)}) async-start(s32[8,1,1]{2,1,0:T(1,128)} %all_to_all.20), calls=%async_computation.2 | async-start | bytes 8192 | tf_op jit(solution)/shard_map/all_to_all | solution.py:78
  16.3 13.3 %all-to-all-start = ((bf16[8,8,3072]{2,1,0:T(8,128)(2,1)}), bf16[8,8,3072]{2,1,0:T(8,128)(2,1)S(1)}, u32[]{:S(2)}, u32[]{:S(2)}) async-start(bf16[8,8,3072]{2,1,0:T(8,128)(2,1)} %bitcast.5), calls=%async_computation | async-start | bytes 786432 | tf_op jit(solution)/shard_map/all_to_all | solution.py:77
  30.4 17.7 %all-to-all-start.1 = ((bf16[8,8,3072]{2,1,0:T(8,128)(2,1)}), bf16[8,8,3072]{2,1,0:T(8,128)(2,1)S(1)}, u32[]{:S(2)}, u32[]{:S(2)}) async-start(bf16[8,8,3072]{2,1,0:T(8,128)(2,1)} %bitcast.11), calls=%async_computation.1 | async-start | bytes 786432 | tf_op jit(solution)/shard_map/all_to_all | solution.py:76
  92.8 14.2 %all-to-all-start.3 = ((bf16[8,8,3072]{2,1,0:T(8,128)(2,1)}), bf16[8,8,3072]{2,1,0:T(8,128)(2,1)S(1)}, u32[]{:S(2)}, u32[]{:S(2)}) async-start(bf16[8,8,3072]{2,1,0:T(8,128)(2,1)} %fusion.39), calls=%async_computation.3 | async-start | bytes 786432 | tf_op jit(solution)/shard_map/all_to_all | solution.py:91
  108.2 2.3 %copy-start.3 = (bf16[1,128,3072]{2,1,0:T(8,128)(2,1)S(1)}, bf16[1,128,3072]{2,1,0:T(8,128)(2,1)}, u32[]{:S(2)}) copy-start(bf16[1,128,3072]{2,1,0:T(8,128)(2,1)} %param.8) | copy-start | bytes 2359300
  110.5 20.4 %copy-start.1 = (bf16[1,128,3072]{2,1,0:T(8,128)(2,1)S(1)}, bf16[1,128,3072]{2,1,0:T(8,128)(2,1)}, u32[]{:S(2)}) copy-start(bf16[1,128,3072]{2,1,0:T(8,128)(2,1)} %param.7) | copy-start | bytes 2359300
  112.4 17.6 %collective-permute-start = (bf16[1,128,3072]{2,1,0:T(8,128)(2,1)S(1)}, bf16[1,128,3072]{2,1,0:T(8,128)(2,1)S(1)}, u32[]{:S(2)}, u32[]{:S(2)}) collective-permute-start(bf16[1,128,3072]{2,1,0:T(8,128)(2,1)S(1)} %fusion.52), channel_id=1, source_target_pairs={{8,0},{16,8},{24,16},{9,1},{17,9},{25,17},{10,2},{18,10},{26,18},{... | collective-permute-start | bytes 2359304 | tf_op jit(solution)/shard_map/ppermute | solution.py:13
where the time goes:
time: 131 us
  matrix products  59.3 us (45%)
  waiting for transfers between devices  30 us (23%)
  starting transfers between devices  27.5 us (21%)
  local copies, waits for them, and re-layouts  8.41 us (6%)
  other arithmetic  5.42 us (4%)
    dot_general x1, matrix products, hidden_grads(): lax.dot_general(gate_grad, gate_slice, contract, preferred_element_type=j...  20.9 us
    dot_general x1, matrix products, hidden_grads(): lax.dot_general(up_grad, up_slice, contract, preferred_element_type=jnp.f...  13.3 us
    dot_general x1, matrix products, hidden_grads(): lax.dot_general(rows_grad, down_slice, contract, preferred_element_type=j...  12.4 us
    ppermute x1, waiting for transfers between devices, from_behind(): lax.ppermute(value, axis, [(source, source + steps) for source in range(f...  10.8 us
    dot_general x1, matrix products, hidden_grads(): gate_pre = jnp.dot(rows_in, gate_slice, preferred_element_type=jnp.float32)  10.5 us
    all_to_all x1, waiting for transfers between devices, shards(): lax.all_to_all(bound_grads, ('expert', 'dp'), split_axis=0, concat_axis=0...  8.85 us
    all_to_all x1, waiting for transfers between devices, shards(): lax.all_to_all(partial_bf, ('expert', 'dp'), split_axis=0, concat_axis=0,...  8.71 us
    ppermute x1, starting transfers between devices, from_behind(): lax.ppermute(value, axis, [(source, source + steps) for source in range(f...  6.76 us
  transfers between devices with their start and end apart: 5, of which 4 were waited for; matrix products, arithmetic and copies ran while one was open for 13% of the time, Pallas kernels for 0%

commit v1 on v0

v1 whole, which is shorter than its diff:
```python
import functools

import jax
import jax.numpy as jnp
from jax import lax
from jax.experimental import pallas as pl
from jax.experimental.pallas import tpu as pltpu
from jax.sharding import PartitionSpec as P

EF = 2
CAP = 8
MIB = 1 << 20
F32 = jnp.float32
BF16 = jnp.bfloat16
NN = (((1,), (0,)), ((), ()))
NT = (((1,), (1,)), ((), ()))
TN = (((0,), (0,)), ((), ()))
VMEM = pl.BlockSpec(memory_space=pltpu.VMEM)
ANY = pl.BlockSpec(memory_space=pl.ANY)


def dot(a, b, dims):
    return lax.dot_general(a, b, dims, preferred_element_type=F32)


def slot_table(picks, expert):
    count = picks.shape[0]
    chosen = jnp.any(picks == expert, axis=1, keepdims=True)
    rows = lax.broadcasted_iota(jnp.int32, (count, count), 0)
    columns = lax.broadcasted_iota(jnp.int32, (count, count), 1)
    before = (columns < rows).astype(BF16)
    flags = jnp.broadcast_to(chosen, (count, 128)).astype(F32).astype(BF16)
    place = dot(before, flags, NN)[:, :CAP]
    slots = lax.broadcasted_iota(jnp.int32, (count, CAP), 1).astype(F32)
    return jnp.where((place == slots) & chosen, 1.0, 0.0)


def route_body(tokens, grad_out, picks_ref, weights_ref, rows_in, rows_grad):
    picks = picks_ref[...]
    pick_weights = weights_ref[...]
    group = rows_in.shape[0] // EF
    upstream = grad_out[...].astype(F32)
    for expert in range(EF):
        table = slot_table(picks, expert).astype(BF16)
        weight = jnp.sum(jnp.where(picks == expert, pick_weights, 0.0), axis=1, keepdims=True)
        scaled = (weight * upstream).astype(BF16)
        sent_in = dot(table, tokens[...], TN).astype(BF16)
        sent_grad = dot(table, scaled, TN).astype(BF16)
        for member in range(group):
            rows_in[expert * group + member] = sent_in
            rows_grad[expert * group + member] = sent_grad


def act_body(rows_grad, down, act_grad, buffers, sems, *, block):
    hidden = down.shape[0]
    count = hidden // block
    depth = buffers.shape[0]

    def fetch(index):
        slot = index % depth
        return pltpu.make_async_copy(down.at[pl.ds(index * block, block), :], buffers.at[slot], sems.at[slot])

    for index in range(min(depth, count)):
        fetch(index).start()
    for index in range(count):
        fetch(index).wait()
        value = dot(buffers[index % depth], rows_grad[...], NT)
        if index + depth < count:
            fetch(index + depth).start()
        act_grad[:, pl.ds(index * block, block)] = value.T


def back_body(rows_in, act_grad, gate, up, out, total, gates, ups, sems, *, block, chunk):
    slots = act_grad.shape[0]
    width, hidden = gate.shape
    count = hidden // block
    depth = gates.shape[0]

    def fetch(index):
        slot = index % depth
        part = pl.ds(index * block, block)
        return (
            pltpu.make_async_copy(gate.at[:, part], gates.at[slot], sems.at[0, slot]),
            pltpu.make_async_copy(up.at[:, part], ups.at[slot], sems.at[1, slot]),
        )

    for index in range(min(depth, count)):
        for copy in fetch(index):
            copy.start()
    for index in range(count):
        part = pl.ds(index * block, block)
        slot = index % depth
        copies = fetch(index)
        copies[0].wait()
        gate_pre = dot(rows_in[...], gates[slot], NN)[:slots]
        copies[1].wait()
        up_pre = dot(rows_in[...], ups[slot], NN)[:slots]
        sigmoid = jax.nn.sigmoid(gate_pre)
        grad = act_grad[:, part]
        gate_grad = (grad * up_pre * sigmoid * (1.0 + gate_pre * (1.0 - sigmoid))).astype(BF16)
        up_grad = (grad * gate_pre * sigmoid).astype(BF16)
        for start in range(0, width, chunk):
            rows = pl.ds(start, chunk)
            value = dot(gates[slot, rows, :], gate_grad, NT) + dot(ups[slot, rows, :], up_grad, NT)
            if index > 0:
                value = value + total[rows, :]
            if index < count - 1:
                total[rows, :] = value
            else:
                out[:, rows] = value.T.astype(BF16)
        if index + depth < count:
            for copy in fetch(index + depth):
                copy.start()


def total_body(parts, total):
    group = parts.shape[0] // EF
    for expert in range(EF):
        value = parts[expert * group].astype(F32)
        for member in range(1, group):
            value = value + parts[expert * group + member].astype(F32)
        total[pl.ds(expert * CAP, CAP), :] = value


def place_body(base, picks_ref, total, out):
    picks = picks_ref[...]
    table = jnp.concatenate([slot_table(picks, expert) for expert in range(EF)], axis=1)
    branch = lax.dot_general(table, total[...], NN, precision=lax.Precision.HIGHEST, preferred_element_type=F32)
    out[...] = (base[...].astype(F32) + branch).astype(BF16)


def call(body, out_shape, args, in_specs, name, limit, **kwargs):
    single = not isinstance(out_shape, (list, tuple))
    return pl.pallas_call(
        body,
        out_shape=out_shape,
        in_specs=in_specs,
        out_specs=VMEM if single else [VMEM] * len(out_shape),
        name=name,
        compiler_params=pltpu.CompilerParams(vmem_limit_bytes=limit),
        **kwargs,
    )(*args)


def to_previous(value, axis="pipe"):
    count = lax.axis_size(axis)
    return lax.ppermute(value, axis, [(source, source - 1) for source in range(1, count)])


def exchange(value):
    return lax.all_to_all(value, ("expert", "dp"), split_axis=0, concat_axis=0, tiled=True)


def shards(tokens, grad_out, routes, route_weights, gate_weight, up_weight, down_weight):
    members = lax.axis_size("expert") * lax.axis_size("dp")
    inputs, upstream, picks, pick_weights = tokens[0], grad_out[0], routes[0], route_weights[0]
    count, width = inputs.shape
    gate, up, down = gate_weight[0], up_weight[0], down_weight[0]
    hidden = gate.shape[1]
    slots = members * CAP
    shape = jax.ShapeDtypeStruct

    bound = shape((members, CAP, width), BF16)
    sent_in, sent_grad = call(
        route_body, [bound, bound], (inputs, upstream, picks, pick_weights), [VMEM] * 4, "route", 32 * MIB
    )
    rows_grad = exchange(sent_grad).reshape(slots, width)
    rows_in = exchange(sent_in).reshape(slots, width)
    next_upstream = to_previous(upstream)
    next_picks = to_previous(picks)

    rows_in = jnp.pad(rows_in, ((0, max(0, 128 - slots)), (0, 0)))
    block = min(hidden, 512)
    depth = 4
    act_grad = call(
        functools.partial(act_body, block=block),
        shape((slots, hidden), F32),
        (rows_grad, down),
        [VMEM, ANY],
        "act",
        40 * MIB,
        scratch_shapes=[pltpu.VMEM((depth, block, width), BF16), pltpu.SemaphoreType.DMA((depth,))],
    )
    depth = 3
    partial = call(
        functools.partial(back_body, block=block, chunk=512),
        shape((slots, width), BF16),
        (rows_in, act_grad, gate, up),
        [VMEM, VMEM, ANY, ANY],
        "back",
        40 * MIB,
        scratch_shapes=[
            pltpu.VMEM((width, slots), F32),
            pltpu.VMEM((depth, width, block), BF16),
            pltpu.VMEM((depth, width, block), BF16),
            pltpu.SemaphoreType.DMA((2, depth)),
        ],
    )
    returned = exchange(partial.reshape(members, CAP, width))
    total = call(total_body, shape((EF * CAP, width), F32), (returned,), [VMEM], "total", 16 * MIB)
    next_total = to_previous(total)
    out = call(
        place_body, shape((count, width), BF16), (next_upstream, next_picks, next_total), [VMEM] * 3, "place", 16 * MIB
    )
    return out[None]


def solution(mesh):
    row = P("pipe", ("expert", "dp"), None)
    column = P("pipe", None, ("expert", "dp"))
    return jax.shard_map(
        shards,
        mesh=mesh,
        in_specs=(row, row, row, row, column, column, row),
        out_specs=row,
        check_vma=False,
    )
```

time: 131 us -> 107 us (0.82)
  matrix products: 59.3 us -> 0 us
  Pallas kernels: 0 us -> 46.5 us
  blocking collectives: 0 us -> 17 us
  waiting for transfers between devices: 30 us -> 16.7 us
  other arithmetic: 5.42 us -> 0 us
  starting transfers between devices: 27.5 us -> 22.5 us
  local copies, waits for them, and re-layouts: 8.41 us -> 3.89 us
    dot_general x8 -> x0, matrix products: 59.3 us -> none  [the longest x1 20.9 us: hidden_grads(): lax.dot_general(gate_grad, gate_slice, contract, preferred_element_type=j...]
    pallas_call x0 -> x5, Pallas kernels: none -> 46.5 us  [call(): pl.pallas_call(body, out_shape=out_shape, in_specs=in_specs, out_specs=VM...]
    all_to_all x0 -> x1, blocking collectives: none -> 17 us  [exchange(): lax.all_to_all(value, ('expert', 'dp'), split_axis=0, concat_axis=0, tile...]
    all_to_all x4 -> x2, starting transfers between devices: 20.8 us -> 9.08 us  [exchange(): lax.all_to_all(value, ('expert', 'dp'), split_axis=0, concat_axis=0, tile...]
    ppermute x1 -> x3, waiting for transfers between devices: 10.8 us -> 3.66 us  [to_previous(): lax.ppermute(value, axis, [(source, source - 1) for source in range(1, co...]
    ppermute x1 -> x3, starting transfers between devices: 6.76 us -> 13.4 us  [to_previous(): lax.ppermute(value, axis, [(source, source - 1) for source in range(1, co...]
    all_to_all x4 -> x2, waiting for transfers between devices: 19.2 us -> 13.1 us  [exchange(): lax.all_to_all(value, ('expert', 'dp'), split_axis=0, concat_axis=0, tile...]
    gather x2 -> x0, local copies, waits for them, and re-layouts: 3.43 us -> none  [shards(): picked_rows = summed[expert][slot_places[expert]]]
  transfers between devices with their start and end apart: 5 -> 5, of which waited for: 4 -> 3; matrix products, arithmetic and copies ran while one was open for 13% -> 0% of each run, Pallas kernels for 0% -> 0%
where the time goes in v1:
time: 107 us
  Pallas kernels  46.5 us (43%)
  starting transfers between devices  22.5 us (21%)
  blocking collectives  17 us (16%)
  waiting for transfers between devices  16.7 us (16%)
  local copies, waits for them, and re-layouts  3.89 us (4%)
    pallas_call x5, Pallas kernels, call(): pl.pallas_call(body, out_shape=out_shape, in_specs=in_specs, out_specs=VM...  46.5 us
    all_to_all x1, blocking collectives, exchange(): lax.all_to_all(value, ('expert', 'dp'), split_axis=0, concat_axis=0, tile...  17 us
    ppermute x3, starting transfers between devices, to_previous(): lax.ppermute(value, axis, [(source, source - 1) for source in range(1, co...  13.4 us
    all_to_all x2, waiting for transfers between devices, exchange(): lax.all_to_all(value, ('expert', 'dp'), split_axis=0, concat_axis=0, tile...  13.1 us
    all_to_all x2, starting transfers between devices, exchange(): lax.all_to_all(value, ('expert', 'dp'), split_axis=0, concat_axis=0, tile...  9.08 us
    unnamed x8, local copies, waits for them, and re-layouts  3.84 us
    ppermute x3, waiting for transfers between devices, to_previous(): lax.ppermute(value, axis, [(source, source - 1) for source in range(1, co...  3.66 us
  transfers between devices with their start and end apart: 5, of which 3 were waited for; matrix products, arithmetic and copies ran while one was open for 0% of the time, Pallas kernels for 0%

profile of v1, /device:TPU:1, one launch (start us, length us, event | category | flops | bytes accessed | tf_op | source)
XLA Modules:
  0.0 106.7 jit_solution(2430184296002413415)
XLA Ops:
  0.0 0.8 copy.8
  0.8 0.8 copy.9
  1.6 0.0 copy-start
  1.6 1.1 %copy-done = bf16[1,128,3072]{2,1,0:T(8,128)(2,1)S(1)} copy-done((bf16[1,128,3072]{2,1,0:T(8,128)(2,1)S(1)}, bf16[1,128,3072]{2,1,0:T(8,128)(2,1)}, u32[]{:S(2)}) %copy-start) | copy-done | bytes 786456
  2.7 0.0 copy-start.1
  2.7 1.1 %copy-done.1 = bf16[1,128,3072]{2,1,0:T(8,128)(2,1)S(1)} copy-done((bf16[1,128,3072]{2,1,0:T(8,128)(2,1)S(1)}, bf16[1,128,3072]{2,1,0:T(8,128)(2,1)}, u32[]{:S(2)}) %copy-start.1) | copy-done | bytes 786456
  3.8 1.7 %route.1 = (bf16[8,8,3072]{2,1,0:T(8,128)(2,1)S(1)}, bf16[8,8,3072]{2,1,0:T(8,128)(2,1)}) custom-call(bf16[128,3072]{1,0:T(8,128)(2,1)S(1)} %bitcast.12, bf16[128,3072]{1,0:T(8,128)(2,1)S(1)} %bitcast.13, s32[128,2]{1,0:T(8,128)S(1)} %bitcast.15, f32[128,2]{1,0:T(8,128)S(1)} %bitcast.17), custom_call_target="tpu_custom_call" | custom-call | tf_op jit(solution)/shard_map/route/pallas_call | solution.py:134
  5.6 17.0 %all_to_all.15 = bf16[8,8,3072]{2,1,0:T(8,128)(2,1)S(1)} all-to-all(bf16[8,8,3072]{2,1,0:T(8,128)(2,1)S(1)} %get-tuple-element.7), channel_id=1, replica_groups=mesh['pipe'=4,'expert'=2,'dp'=4] {'expert','dp'}, dimensions={0} | all-to-all | bytes 786432 | tf_op jit(solution)/shard_map/all_to_all | solution.py:151
  22.6 4.0 %all-to-all-start.1 = ((bf16[8,8,3072]{2,1,0:T(8,128)(2,1)}), bf16[8,8,3072]{2,1,0:T(8,128)(2,1)S(1)}, u32[]{:S(2)}, u32[]{:S(2)}) async-start(bf16[8,8,3072]{2,1,0:T(8,128)(2,1)} %get-tuple-element.8), calls=%async_computation.1 | async-start | bytes 786432 | tf_op jit(solution)/shard_map/all_to_all | solution.py:151
  26.6 0.1 pad.4.rows_in
  26.6 9.0 %all-to-all-done.1 = bf16[8,8,3072]{2,1,0:T(8,128)(2,1)S(1)} async-done(((bf16[8,8,3072]{2,1,0:T(8,128)(2,1)}), bf16[8,8,3072]{2,1,0:T(8,128)(2,1)S(1)}, u32[]{:S(2)}, u32[]{:S(2)}) %all-to-all-start.1) | async-done | bytes 393248 | tf_op jit(solution)/shard_map/all_to_all | solution.py:151
  35.7 16.3 %act.1.act_grad = f32[64,4096]{1,0:T(8,128)S(1)} custom-call(bf16[64,3072]{1,0:T(8,128)(2,1)S(1)} %bitcast.11, bf16[4096,3072]{1,0:T(8,128)(2,1)} %bitcast.18), custom_call_target="tpu_custom_call" | custom-call | tf_op jit(solution)/shard_map/act/pallas_call | solution.py:134
  52.0 0.0 copy-start.2
  52.0 25.9 %back.1 = bf16[64,3072]{1,0:T(8,128)(2,1)} custom-call(bf16[128,3072]{1,0:T(8,128)(2,1)S(1)} %pad.4.rows_in, f32[64,4096]{1,0:T(8,128)S(1)} %act.1.act_grad, bf16[3072,4096]{1,0:T(8,128)(2,1)} %bitcast.19, bf16[3072,4096]{1,0:T(8,128)(2,1)} %bitcast.20), custom_call_target="tpu_custom_call" | custom-call | tf_op jit(solution)/shard_map/back/pallas_call | solution.py:134
  77.9 5.1 %all-to-all-start.2 = ((bf16[8,8,3072]{2,1,0:T(8,128)(2,1)}), bf16[8,8,3072]{2,1,0:T(8,128)(2,1)S(1)}, u32[]{:S(2)}, u32[]{:S(2)}) async-start(bf16[8,8,3072]{2,1,0:T(8,128)(2,1)} %bitcast.9), calls=%async_computation.2 | async-start | bytes 786432 | tf_op jit(solution)/shard_map/all_to_all | solution.py:151
  83.0 0.0 copy-done.2
  83.0 4.7 %collective-permute-start = (bf16[128,3072]{1,0:T(8,128)(2,1)S(1)}, bf16[128,3072]{1,0:T(8,128)(2,1)S(1)}, u32[]{:S(2)}, u32[]{:S(2)}) collective-permute-start(bf16[128,3072]{1,0:T(8,128)(2,1)S(1)} %bitcast.14), channel_id=1, source_target_pairs={{8,0},{16,8},{24,16},{9,1},{17,9},{25,17},{10,2},{18,10},{26,18},{... | collective-permute-start | bytes 2359304 | tf_op jit(solution)/shard_map/ppermute | solution.py:147
  87.7 4.0 %all-to-all-done.2.parts = bf16[8,8,3072]{2,1,0:T(8,128)(2,1)S(1)} async-done(((bf16[8,8,3072]{2,1,0:T(8,128)(2,1)}), bf16[8,8,3072]{2,1,0:T(8,128)(2,1)S(1)}, u32[]{:S(2)}, u32[]{:S(2)}) %all-to-all-start.2) | async-done | bytes 393248 | tf_op jit(solution)/shard_map/all_to_all | solution.py:151
  91.8 6.8 %collective-permute-start.2 = (f32[16,3072]{1,0:T(8,128)S(1)}, f32[16,3072]{1,0:T(8,128)S(1)}, u32[]{:S(2)}, u32[]{:S(2)}) collective-permute-start(f32[16,3072]{1,0:T(8,128)S(1)} %total.1), channel_id=1, source_target_pairs={{8,0},{16,8},{24,16},{9,1},{17,9},{25,17},{10,2},{18,10},{26,18},{... | collective-permute-start | bytes 589832 | tf_op jit(solution)/shard_map/ppermute | solution.py:147
  98.6 1.9 %collective-permute-start.1 = (s32[128,2]{1,0:T(8,128)S(1)}, s32[128,2]{1,0:T(8,128)S(1)}, u32[]{:S(2)}, u32[]{:S(2)}) collective-permute-start(s32[128,2]{1,0:T(8,128)S(1)} %bitcast.16), channel_id=1, source_target_pairs={{8,0},{16,8},{24,16},{9,1},{17,9},{25,17},{10,2},{18,10},{26,18},{... | collective-permute-start | bytes 3080 | tf_op jit(solution)/shard_map/ppermute | solution.py:147
  100.5 3.7 %collective-permute-done.1.picks_ref = s32[128,2]{1,0:T(8,128)S(1)} collective-permute-done((s32[128,2]{1,0:T(8,128)S(1)}, s32[128,2]{1,0:T(8,128)S(1)}, u32[]{:S(2)}, u32[]{:S(2)}) %collective-permute-start.1) | collective-permute-done | bytes 1056 | tf_op jit(solution)/shard_map/ppermute | solution.py:147
  104.2 0.0 collective-permute-done.base
  104.2 0.0 collective-permute-done.2.total
  104.2 2.5 %place.1 = bf16[128,3072]{1,0:T(8,128)(2,1)} custom-call(bf16[128,3072]{1,0:T(8,128)(2,1)S(1)} %collective-permute-done.base, s32[128,2]{1,0:T(8,128)S(1)} %collective-permute-done.1.picks_ref, f32[16,3072]{1,0:T(8,128)S(1)} %collective-permute-done.2.total), custom_call_target="tpu_custom_call" | custom-call | tf_op jit(solution)/shard_map/place/pallas_call | solution.py:134
  (1 shorter events, 0.0 us)
Async XLA Ops:
  1.6 1.1 %copy-start = (bf16[1,128,3072]{2,1,0:T(8,128)(2,1)S(1)}, bf16[1,128,3072]{2,1,0:T(8,128)(2,1)}, u32[]{:S(2)}) copy-start(bf16[1,128,3072]{2,1,0:T(8,128)(2,1)} %param.7) | copy-start | bytes 2359300
  2.7 1.1 %copy-start.1 = (bf16[1,128,3072]{2,1,0:T(8,128)(2,1)S(1)}, bf16[1,128,3072]{2,1,0:T(8,128)(2,1)}, u32[]{:S(2)}) copy-start(bf16[1,128,3072]{2,1,0:T(8,128)(2,1)} %param.8) | copy-start | bytes 2359300
  22.6 13.1 %all-to-all-start.1 = ((bf16[8,8,3072]{2,1,0:T(8,128)(2,1)}), bf16[8,8,3072]{2,1,0:T(8,128)(2,1)S(1)}, u32[]{:S(2)}, u32[]{:S(2)}) async-start(bf16[8,8,3072]{2,1,0:T(8,128)(2,1)} %get-tuple-element.8), calls=%async_computation.1 | async-start | bytes 786432 | tf_op jit(solution)/shard_map/all_to_all | solution.py:151
  52.0 31.0 %copy-start.2 = (bf16[1,128,3072]{2,1,0:T(8,128)(2,1)S(1)}, bf16[1,128,3072]{2,1,0:T(8,128)(2,1)}, u32[]{:S(2)}) copy-start(bf16[1,128,3072]{2,1,0:T(8,128)(2,1)} %param.8) | copy-start | bytes 2359300
  77.9 13.9 %all-to-all-start.2 = ((bf16[8,8,3072]{2,1,0:T(8,128)(2,1)}), bf16[8,8,3072]{2,1,0:T(8,128)(2,1)S(1)}, u32[]{:S(2)}, u32[]{:S(2)}) async-start(bf16[8,8,3072]{2,1,0:T(8,128)(2,1)} %bitcast.9), calls=%async_computation.2 | async-start | bytes 786432 | tf_op jit(solution)/shard_map/all_to_all | solution.py:151
  83.0 21.1 %collective-permute-start = (bf16[128,3072]{1,0:T(8,128)(2,1)S(1)}, bf16[128,3072]{1,0:T(8,128)(2,1)S(1)}, u32[]{:S(2)}, u32[]{:S(2)}) collective-permute-start(bf16[128,3072]{1,0:T(8,128)(2,1)S(1)} %bitcast.14), channel_id=1, source_target_pairs={{8,0},{16,8},{24,16},{9,1},{17,9},{25,17},{10,2},{18,10},{26,18},{... | collective-permute-start | bytes 2359304 | tf_op jit(solution)/shard_map/ppermute | solution.py:147
  91.8 12.4 %collective-permute-start.2 = (f32[16,3072]{1,0:T(8,128)S(1)}, f32[16,3072]{1,0:T(8,128)S(1)}, u32[]{:S(2)}, u32[]{:S(2)}) collective-permute-start(f32[16,3072]{1,0:T(8,128)S(1)} %total.1), channel_id=1, source_target_pairs={{8,0},{16,8},{24,16},{9,1},{17,9},{25,17},{10,2},{18,10},{26,18},{... | collective-permute-start | bytes 589832 | tf_op jit(solution)/shard_map/ppermute | solution.py:147
  98.6 5.6 %collective-permute-start.1 = (s32[128,2]{1,0:T(8,128)S(1)}, s32[128,2]{1,0:T(8,128)S(1)}, u32[]{:S(2)}, u32[]{:S(2)}) collective-permute-start(s32[128,2]{1,0:T(8,128)S(1)} %bitcast.16), channel_id=1, source_target_pairs={{8,0},{16,8},{24,16},{9,1},{17,9},{25,17},{10,2},{18,10},{26,18},{... | collective-permute-start | bytes 3080 | tf_op jit(solution)/shard_map/ppermute | solution.py:147

commit v2 on v1

v2 whole, which is shorter than its diff:
```python
import functools

import jax
import jax.numpy as jnp
from jax import lax
from jax.experimental import pallas as pl
from jax.experimental.pallas import tpu as pltpu
from jax.sharding import PartitionSpec as P

EF = 2
CAP = 8
MIB = 1 << 20
F32 = jnp.float32
BF16 = jnp.bfloat16
NN = (((1,), (0,)), ((), ()))
NT = (((1,), (1,)), ((), ()))
TN = (((0,), (0,)), ((), ()))
VMEM = pl.BlockSpec(memory_space=pltpu.VMEM)
SMEM = pl.BlockSpec(memory_space=pltpu.SMEM)
HBM = pl.BlockSpec(memory_space=pltpu.HBM)
AXES = ("pipe", "expert", "dp")


def dot(a, b, dims):
    return lax.dot_general(a, b, dims, preferred_element_type=F32)


def slot_table(picks, expert):
    count = picks.shape[1]
    chosen = (picks[0:1, :] == expert) | (picks[1:2, :] == expert)
    rows = lax.broadcasted_iota(jnp.int32, (count, count), 0)
    columns = lax.broadcasted_iota(jnp.int32, (count, count), 1)
    before = jnp.where(rows < columns, 1.0, 0.0).astype(BF16)
    flags = jnp.broadcast_to(jnp.where(chosen, 1.0, 0.0), (CAP, count))
    place = dot(flags.astype(BF16), before, NN)
    slots = lax.broadcasted_iota(jnp.int32, (CAP, count), 0).astype(F32)
    return jnp.where(place == slots, flags, 0.0)


def pick_weight(picks, pick_weights, expert):
    first = jnp.where(picks[0:1, :] == expert, pick_weights[0:1, :], 0.0)
    return first + jnp.where(picks[1:2, :] == expert, pick_weights[1:2, :], 0.0)


def select(experts, picks, pick_weights, tokens, upstream):
    tables = [slot_table(picks, expert) for expert in experts]
    weights = [
        jnp.sum(table * pick_weight(picks, pick_weights, expert), axis=1, keepdims=True)
        for table, expert in zip(tables, experts)
    ]
    table = jnp.concatenate(tables, axis=0).astype(BF16)
    sent_in = dot(table, tokens, NN).astype(BF16)
    sent_grad = (jnp.concatenate(weights, axis=0) * dot(table, upstream, NN)).astype(BF16)
    return sent_in, sent_grad


def load(sources, targets, sems):
    copies = [
        pltpu.make_async_copy(source, target, sems.at[index])
        for index, (source, target) in enumerate(zip(sources, targets))
    ]
    for copy in copies:
        copy.start()
    for copy in copies:
        copy.wait()
    return [target[...] for target in targets]


def route_body(own, picks, pick_weights, tokens, grad_out, kept_in, kept_grad, sent, *scratch):
    loaded = load((picks, pick_weights, tokens, grad_out), scratch[:-1], scratch[-1])
    first = own[0]
    rows_in, rows_grad = select((first, 1 - first), *loaded)
    kept_in[...] = rows_in[:CAP]
    kept_grad[...] = rows_grad[:CAP]
    sent[0] = rows_grad[CAP:]
    sent[1] = rows_in[CAP:]


def route_all_body(picks, pick_weights, tokens, grad_out, rows_in, rows_grad, *scratch):
    loaded = load((picks, pick_weights, tokens, grad_out), scratch[:-1], scratch[-1])
    sent_in, sent_grad = select(range(EF), *loaded)
    group = rows_in.shape[0] // EF
    for expert in range(EF):
        for member in range(group):
            rows_in[expert * group + member] = sent_in[expert * CAP : (expert + 1) * CAP]
            rows_grad[expert * group + member] = sent_grad[expert * CAP : (expert + 1) * CAP]


def join_body(kept_in, kept_grad, received, rows_in, rows_grad):
    rows_in[...] = jnp.concatenate([kept_in[...], received[1]], axis=0)
    rows_grad[...] = jnp.concatenate([kept_grad[...], received[0]], axis=0)


def act_body(*refs, pieces, block):
    down, act_grad, rows, buffers, sems = refs[pieces:]
    hidden = down.shape[0]
    count = hidden // block
    depth = buffers.shape[0]

    def fetch(index):
        slot = index % depth
        return pltpu.make_async_copy(down.at[pl.ds(index * block, block), :], buffers.at[slot], sems.at[slot])

    for index in range(min(depth, count)):
        fetch(index).start()
    gather(refs[:pieces], rows)
    for index in range(count):
        fetch(index).wait()
        act_grad[:, pl.ds(index * block, block)] = dot(rows[...], buffers[index % depth], NT)
        if index + depth < count:
            fetch(index + depth).start()


def gather(pieces, rows):
    start = 0
    for piece in pieces:
        size = piece.shape[0]
        rows[pl.ds(start, size), :] = piece[...]
        start += size
    if start < rows.shape[0]:
        rows[pl.ds(start, rows.shape[0] - start), :] = jnp.zeros((rows.shape[0] - start, rows.shape[1]), BF16)


def back_body(*refs, pieces, block, chunk, kept):
    act_grad, gate, up = refs[pieces : pieces + 3]
    outs = refs[pieces + 3 : 2 * pieces + 3]
    rows_in, total, *buffers, sems = refs[2 * pieces + 3 :]
    slots = act_grad.shape[0]
    size = slots // pieces
    width, hidden = gate.shape
    count = hidden // block
    depth = buffers[0].shape[0]
    sources = ((up,) if kept else (up, gate))

    def fetch(index):
        slot = index % depth
        part = pl.ds(index * block, block)
        return [
            pltpu.make_async_copy(source.at[:, part], buffer.at[slot], sems.at[order, slot])
            for order, (source, buffer) in enumerate(zip(sources, buffers))
        ]

    for index in range(min(depth, count)):
        for copy in reversed(fetch(index)):
            copy.start()
    gather(refs[:pieces], rows_in)
    for index in range(count):
        part = pl.ds(index * block, block)
        slot = index % depth
        copies = fetch(index)
        if kept:
            gates = gate.at[:, part]
        else:
            copies[1].wait()
            gates = buffers[1].at[slot]
        ups = buffers[0].at[slot]
        gate_pre = dot(rows_in[...], gates[...], NN)[:slots]
        copies[0].wait()
        up_pre = dot(rows_in[...], ups[...], NN)[:slots]
        sigmoid = jax.nn.sigmoid(gate_pre)
        grad = act_grad[:, part]
        gate_grad = (grad * up_pre * sigmoid * (1.0 + gate_pre * (1.0 - sigmoid))).astype(BF16)
        up_grad = (grad * gate_pre * sigmoid).astype(BF16)
        for start in range(0, width, chunk):
            rows = pl.ds(start, chunk)
            value = dot(gates[rows, :], gate_grad, NT) + dot(ups[rows, :], up_grad, NT)
            if index > 0:
                value = value + total[rows, :]
            if index < count - 1:
                total[rows, :] = value
            else:
                value = value.T.astype(BF16)
                for piece in range(pieces):
                    outs[piece][:, rows] = value[piece * size : (piece + 1) * size]
        if index + depth < count:
            for copy in reversed(fetch(index + depth)):
                copy.start()


def sum_body(*refs):
    kept, sent = refs[-2:]
    value = refs[0][...].astype(F32)
    for part in refs[1:-2]:
        value = value + part[...].astype(F32)
    kept[...] = value[:CAP]
    sent[...] = value[CAP:]


def sum_all_body(parts, first, second):
    group = parts.shape[0] // EF
    for expert, total in enumerate((first, second)):
        value = parts[expert * group].astype(F32)
        for member in range(1, group):
            value = value + parts[expert * group + member].astype(F32)
        total[...] = value


def place_body(own, base, picks, kept, received, out):
    first = own[0]
    table = jnp.concatenate([slot_table(picks[...], first), slot_table(picks[...], 1 - first)], axis=0)
    total = jnp.concatenate([kept[...], received[...]], axis=0)
    branch = lax.dot_general(table, total, TN, precision=lax.Precision.HIGHEST, preferred_element_type=F32)
    out[...] = (base[...].astype(F32) + branch).astype(BF16)


def hold_body(source, target, sem):
    copy = pltpu.make_async_copy(source, target, sem)
    copy.start()
    copy.wait()


def hold(value):
    return call(
        hold_body,
        pltpu.VMEM(value.shape, value.dtype),
        (value,),
        [HBM],
        "hold",
        1 * MIB,
        scratch_shapes=[pltpu.SemaphoreType.DMA],
    )


def resident(value):
    return pltpu.with_memory_space_constraint(value, pltpu.VMEM)


def call(body, out_shape, args, in_specs, name, limit, **kwargs):
    single = not isinstance(out_shape, (list, tuple))
    args = [
        pltpu.with_memory_space_constraint(arg, pltpu.HBM) if spec is HBM else arg
        for arg, spec in zip(args, in_specs)
    ]
    specs = VMEM if single else [VMEM] * len(out_shape)
    return pl.pallas_call(
        body,
        out_shape=out_shape,
        in_specs=in_specs,
        out_specs=kwargs.pop("out_specs", specs),
        name=name,
        compiler_params=pltpu.CompilerParams(vmem_limit_bytes=limit),
        **kwargs,
    )(*args)


def send(value, target, first=1):
    sizes = [lax.axis_size(axis) for axis in AXES]
    pairs = []
    for pipe in range(first, sizes[0]):
        for expert in range(sizes[1]):
            for data in range(sizes[2]):
                where = target(pipe, expert, data)
                pairs.append(tuple((p * sizes[1] + e) * sizes[2] + d for p, e, d in ((pipe, expert, data), where)))
    return lax.ppermute(value, AXES, pairs)


def to_previous(value):
    return send(value, lambda p, e, d: (p - 1, e, d))


def exchange(value):
    return lax.all_to_all(value, ("expert", "dp"), split_axis=0, concat_axis=0, tiled=True)


def shards(tokens, grad_out, routes, route_weights, gate_weight, up_weight, down_weight):
    members = lax.axis_size("expert") * lax.axis_size("dp")
    lines = lax.axis_size("dp")
    paired = lax.axis_size("expert") == EF and lines & (lines - 1) == 0
    inputs, upstream = tokens[0], grad_out[0]
    picks, pick_weights = routes[0].T, route_weights[0].T
    count, width = inputs.shape
    gate, up, down = gate_weight[0], up_weight[0], down_weight[0]
    hidden = gate.shape[1]
    slots = members * CAP
    shape = jax.ShapeDtypeStruct
    own = lax.axis_index("expert").astype(jnp.int32).reshape(1) if paired else jnp.zeros((1,), jnp.int32)
    sources = (picks, pick_weights, inputs, upstream)
    staging = [pltpu.VMEM(source.shape, source.dtype) for source in sources] + [pltpu.SemaphoreType.DMA((4,))]

    if paired:
        eight = shape((CAP, width), BF16)
        kept_in, kept_grad, sent = call(
            route_body,
            [eight, eight, shape((2, CAP, width), BF16)],
            (own, *sources),
            [SMEM] + [HBM] * 4,
            "route",
            16 * MIB,
            scratch_shapes=staging,
        )
        sent, picks, upstream = lax.optimization_barrier((sent, picks, upstream))
        received = send(sent, lambda p, e, d: (p, 1 - e, d))
        next_upstream = to_previous(upstream)
        next_picks = to_previous(picks)
        sixteen = shape((EF * CAP, width), BF16)
        near_in, near_grad = call(
            join_body, [sixteen, sixteen], (kept_in, kept_grad, received), [VMEM] * 3, "join", 8 * MIB
        )
        order = [step for step in reversed(range(1, lines))]
        far_grad = [send(near_grad, lambda p, e, d, step=step: (p, e, d ^ step)) for step in order]
        far_in = [send(near_in, lambda p, e, d, step=step: (p, e, d ^ step)) for step in order]
        grad_pieces = [near_grad] + far_grad
        in_pieces = [near_in] + far_in
        near_grad, gate = lax.optimization_barrier((near_grad, gate))
        gate = hold(gate)
        grad_pieces, next_picks, gate = lax.optimization_barrier((grad_pieces, next_picks, gate))
    else:
        bound = shape((members, CAP, width), BF16)
        sent_in, sent_grad = call(
            route_all_body,
            [bound, bound],
            sources,
            [HBM] * 4,
            "route",
            32 * MIB,
            scratch_shapes=staging,
        )
        grad_pieces = [exchange(sent_grad).reshape(slots, width)]
        in_pieces = [exchange(sent_in).reshape(slots, width)]
        next_upstream = to_previous(upstream)
        next_picks = to_previous(picks)

    pieces = len(in_pieces)
    block = min(hidden, 512)
    depth = 3
    act_grad = call(
        functools.partial(act_body, pieces=pieces, block=block),
        shape((slots, hidden), F32),
        (*grad_pieces, down),
        [VMEM] * pieces + [HBM],
        "act",
        14 * MIB,
        scratch_shapes=[
            pltpu.VMEM((slots, width), BF16),
            pltpu.VMEM((depth, block, width), BF16),
            pltpu.SemaphoreType.DMA((depth,)),
        ],
    )
    depth = 3
    partial = call(
        functools.partial(back_body, pieces=pieces, block=block, chunk=512, kept=paired),
        [shape((slots // pieces, width), BF16)] * pieces,
        (*in_pieces, act_grad, resident(gate) if paired else gate, up),
        [VMEM] * (pieces + 1) + [VMEM if paired else HBM, HBM],
        "back",
        (20 if paired else 40) * MIB,
        scratch_shapes=[
            pltpu.VMEM((max(128, slots), width), BF16),
            pltpu.VMEM((width, slots), F32),
            *[pltpu.VMEM((depth, width, block), BF16)] * (1 if paired else 2),
            pltpu.SemaphoreType.DMA((2, depth)),
        ],
    )
    total = shape((CAP, width), F32)
    if paired:
        steps = order + [0]
        given = partial[1:] + partial[:1]
        parts = [send(part, lambda p, e, d, step=step: (p - 1, e, d ^ step)) for part, step in zip(given, steps)]
        kept, sent = call(sum_body, [total, total], parts, [VMEM] * pieces, "sum", 16 * MIB)
        received = send(sent, lambda p, e, d: (p, 1 - e, d), first=0)
    else:
        returned = exchange(partial[0].reshape(members, CAP, width))
        kept, received = map(
            to_previous, call(sum_all_body, [total, total], (returned,), [VMEM], "sum", 16 * MIB)
        )
    columns = 768
    out = call(
        place_body,
        shape((count, width), BF16),
        (own, next_upstream, next_picks, kept, received),
        [
            SMEM,
            pl.BlockSpec((count, columns), lambda i: (0, i)),
            pl.BlockSpec(picks.shape, lambda i: (0, 0)),
            pl.BlockSpec((CAP, columns), lambda i: (0, i)),
            pl.BlockSpec((CAP, columns), lambda i: (0, i)),
        ],
        "place",
        16 * MIB,
        grid=(width // columns,),
        out_specs=pl.BlockSpec((count, columns), lambda i: (0, i)),
    )
    return out[None]


def solution(mesh):
    row = P("pipe", ("expert", "dp"), None)
    column = P("pipe", None, ("expert", "dp"))
    return jax.shard_map(
        shards,
        mesh=mesh,
        in_specs=(row, row, row, row, column, column, row),
        out_specs=row,
        check_vma=False,
    )
```

time: 107 us -> 99 us (0.925)
  blocking collectives: 17 us -> 0 us
  starting transfers between devices: 22.5 us -> 36.3 us
  local copies, waits for them, and re-layouts: 3.89 us -> 0 us
  waiting for transfers between devices: 16.7 us -> 14.6 us
    ppermute x3 -> x14, starting transfers between devices: 13.4 us -> 36.3 us  [send(): return lax.ppermute(value, AXES, pairs)]
    all_to_all x1 -> x0, blocking collectives: 17 us -> none  [exchange(): lax.all_to_all(value, ('expert', 'dp'), split_axis=0, concat_axis=0, tile...]
    all_to_all x2 -> x0, waiting for transfers between devices: 13.1 us -> none  [exchange(): lax.all_to_all(value, ('expert', 'dp'), split_axis=0, concat_axis=0, tile...]
    ppermute x3 -> x14, waiting for transfers between devices: 3.66 us -> 14.6 us  [send(): return lax.ppermute(value, AXES, pairs)]
    all_to_all x2 -> x0, starting transfers between devices: 9.08 us -> none  [exchange(): lax.all_to_all(value, ('expert', 'dp'), split_axis=0, concat_axis=0, tile...]
    unnamed x8 -> x0, local copies, waits for them, and re-layouts: 3.84 us -> none
    pallas_call x5 -> x7, Pallas kernels: 46.5 us -> 47.4 us  [call(): pl.pallas_call(body, out_shape=out_shape, in_specs=in_specs, out_specs=kw...]
  transfers between devices with their start and end apart: 5 -> 14, of which waited for: 3 -> 6; matrix products, arithmetic and copies ran while one was open for 0% -> 0% of each run, Pallas kernels for 0% -> 43%
where the time goes in v2:
time: 99 us; the launch traced here: 98.5 us
  Pallas kernels  47.4 us (48%)
  starting transfers between devices  36.3 us (37%)
  waiting for transfers between devices  14.6 us (15%)
    pallas_call x7, Pallas kernels, call(): pl.pallas_call(body, out_shape=out_shape, in_specs=in_specs, out_specs=kw...  47.4 us
    ppermute x14, starting transfers between devices, send(): return lax.ppermute(value, AXES, pairs)  36.3 us
    ppermute x14, waiting for transfers between devices, send(): return lax.ppermute(value, AXES, pairs)  14.6 us
  transfers between devices with their start and end apart: 14, of which 6 were waited for; matrix products, arithmetic and copies ran while one was open for 0% of the time, Pallas kernels for 43%

profile of v2, /device:TPU:1, one launch (start us, length us, event | category | flops | bytes accessed | tf_op | source)
XLA Modules:
  0.0 98.5 jit_solution(14543439491695995029)
XLA Ops:
  0.0 1.9 %route.1 = (bf16[8,3072]{1,0:T(8,128)(2,1)S(1)}, bf16[8,3072]{1,0:T(8,128)(2,1)S(1)}, bf16[2,8,3072]{2,1,0:T(8,128)(2,1)S(1)}) custom-call(s32[1]{0:T(128)} %bitcast.own, s32[2,128]{1,0:T(2,128)} %bitcast.20, f32[2,128]{1,0:T(2,128)} %bitcast.19, bf16[128,3072]{1,0:T(8,128)(2,1)} %bitcast.16, bf16[128,3072]{1,0:T(8,128)(2,1)} %bitcast.17), custom_call_target="tpu_custom_call" | custom-call | tf_op jit(solution)/shard_map/route/pallas_call | solution.py:235
  1.9 2.0 %collective-permute-start = (bf16[128,3072]{1,0:T(8,128)(2,1)}, bf16[128,3072]{1,0:T(8,128)(2,1)S(1)}, u32[]{:S(2)}, u32[]{:S(2)}) collective-permute-start(bf16[128,3072]{1,0:T(8,128)(2,1)} %bitcast.18), channel_id=1, source_target_pairs={{8,0},{9,1},{10,2},{11,3},{12,4},{13,5},{14,6},{15,7},{16,8},{17,9... | collective-permute-start | bytes 2359304 | tf_op jit(solution)/shard_map/ppermute | solution.py:254
  3.9 4.6 %collective-permute-start.1 = (bf16[2,8,3072]{2,1,0:T(8,128)(2,1)S(1)}, bf16[2,8,3072]{2,1,0:T(8,128)(2,1)S(1)}, u32[]{:S(2)}, u32[]{:S(2)}) collective-permute-start(bf16[2,8,3072]{2,1,0:T(8,128)(2,1)S(1)} %get-tuple-element.30), channel_id=1, source_target_pairs={{8,12},{9,13},{10,14},{11,15},{12,8},{13,9},{14,10},{15,11},{16,20... | collective-permute-start | bytes 294920 | tf_op jit(solution)/shard_map/ppermute | solution.py:254
  8.4 2.0 %collective-permute-done.1.received = bf16[2,8,3072]{2,1,0:T(8,128)(2,1)S(1)} collective-permute-done((bf16[2,8,3072]{2,1,0:T(8,128)(2,1)S(1)}, bf16[2,8,3072]{2,1,0:T(8,128)(2,1)S(1)}, u32[]{:S(2)}, u32[]{:S(2)}) %collective-permute-start.1) | collective-permute-done | bytes 98336 | tf_op jit(solution)/shard_map/ppermute | solution.py:254
  10.5 5.5 %collective-permute-start.2 = (bf16[16,3072]{1,0:T(8,128)(2,1)S(1)}, bf16[16,3072]{1,0:T(8,128)(2,1)S(1)}, u32[]{:S(2)}, u32[]{:S(2)}) collective-permute-start(bf16[16,3072]{1,0:T(8,128)(2,1)S(1)} %get-tuple-element.36.refs_0_), channel_id=1, source_target_pairs={{8,11},{9,10},{10,9},{11,8},{12,15},{13,14},{14,13},{15,12},{16,19... | collective-permute-start | bytes 294920 | tf_op jit(solution)/shard_map/ppermute | solution.py:254
  15.9 1.9 %collective-permute-start.3 = (bf16[16,3072]{1,0:T(8,128)(2,1)S(1)}, bf16[16,3072]{1,0:T(8,128)(2,1)S(1)}, u32[]{:S(2)}, u32[]{:S(2)}) collective-permute-start(bf16[16,3072]{1,0:T(8,128)(2,1)S(1)} %get-tuple-element.36.refs_0_), channel_id=1, source_target_pairs={{8,10},{9,11},{10,8},{11,9},{12,14},{13,15},{14,12},{15,13},{16,18... | collective-permute-start | bytes 294920 | tf_op jit(solution)/shard_map/ppermute | solution.py:254
  17.9 1.9 %collective-permute-start.5 = (s32[2,128]{1,0:T(2,128)}, s32[2,128]{1,0:T(2,128)S(1)}, u32[]{:S(2)}, u32[]{:S(2)}) collective-permute-start(s32[2,128]{1,0:T(2,128)} %bitcast.21), channel_id=1, source_target_pairs={{8,0},{9,1},{10,2},{11,3},{12,4},{13,5},{14,6},{15,7},{16,8},{17,9... | collective-permute-start | bytes 3080 | tf_op jit(solution)/shard_map/ppermute | solution.py:254
  19.8 2.2 %collective-permute-start.4 = (bf16[16,3072]{1,0:T(8,128)(2,1)S(1)}, bf16[16,3072]{1,0:T(8,128)(2,1)S(1)}, u32[]{:S(2)}, u32[]{:S(2)}) collective-permute-start(bf16[16,3072]{1,0:T(8,128)(2,1)S(1)} %get-tuple-element.36.refs_0_), channel_id=1, source_target_pairs={{8,9},{9,8},{10,11},{11,10},{12,13},{13,12},{14,15},{15,14},{16,17... | collective-permute-start | bytes 294920 | tf_op jit(solution)/shard_map/ppermute | solution.py:254
  22.0 2.4 %collective-permute-done.5.picks = s32[2,128]{1,0:T(2,128)S(1)} collective-permute-done((s32[2,128]{1,0:T(2,128)}, s32[2,128]{1,0:T(2,128)S(1)}, u32[]{:S(2)}, u32[]{:S(2)}) %collective-permute-start.5) | collective-permute-done | bytes 1056 | tf_op jit(solution)/shard_map/ppermute | solution.py:254
  24.4 3.5 %collective-permute-start.6 = (bf16[16,3072]{1,0:T(8,128)(2,1)S(1)}, bf16[16,3072]{1,0:T(8,128)(2,1)S(1)}, u32[]{:S(2)}, u32[]{:S(2)}) collective-permute-start(bf16[16,3072]{1,0:T(8,128)(2,1)S(1)} %get-tuple-element.35.refs_0_), channel_id=1, source_target_pairs={{8,11},{9,10},{10,9},{11,8},{12,15},{13,14},{14,13},{15,12},{16,19... | collective-permute-start | bytes 294920 | tf_op jit(solution)/shard_map/ppermute | solution.py:254
  28.0 2.9 %collective-permute-start.7 = (bf16[16,3072]{1,0:T(8,128)(2,1)S(1)}, bf16[16,3072]{1,0:T(8,128)(2,1)S(1)}, u32[]{:S(2)}, u32[]{:S(2)}) collective-permute-start(bf16[16,3072]{1,0:T(8,128)(2,1)S(1)} %get-tuple-element.35.refs_0_), channel_id=1, source_target_pairs={{8,10},{9,11},{10,8},{11,9},{12,14},{13,15},{14,12},{15,13},{16,18... | collective-permute-start | bytes 294920 | tf_op jit(solution)/shard_map/ppermute | solution.py:254
  30.9 2.8 %collective-permute-start.8 = (bf16[16,3072]{1,0:T(8,128)(2,1)S(1)}, bf16[16,3072]{1,0:T(8,128)(2,1)S(1)}, u32[]{:S(2)}, u32[]{:S(2)}) collective-permute-start(bf16[16,3072]{1,0:T(8,128)(2,1)S(1)} %get-tuple-element.35.refs_0_), channel_id=1, source_target_pairs={{8,9},{9,8},{10,11},{11,10},{12,13},{13,12},{14,15},{15,14},{16,17... | collective-permute-start | bytes 294920 | tf_op jit(solution)/shard_map/ppermute | solution.py:254
  33.7 8.2 %hold.1.refs_5_ = bf16[3072,4096]{1,0:T(8,128)(2,1)S(1)} custom-call(bf16[3072,4096]{1,0:T(8,128)(2,1)} %bitcast.13), custom_call_target="tpu_custom_call" | custom-call | tf_op jit(solution)/shard_map/hold/pallas_call | solution.py:235
  41.9 10.5 %act.1.refs_4_ = f32[64,4096]{1,0:T(8,128)S(1)} custom-call(bf16[16,3072]{1,0:T(8,128)(2,1)S(1)} %get-tuple-element.36.refs_0_, bf16[16,3072]{1,0:T(8,128)(2,1)S(1)} %collective-permute-done.2.refs_1_, bf16[16,3072]{1,0:T(8,128)(2,1)S(1)} %collective-permute-done.3.refs_2_, bf16[16,3072]{1,0:T(8,128)(2,1)S(1)} %collective-permute-done.4.refs_3_, ...), custom_call_target="tpu_custom_call" | custom-call | tf_op jit(solution)/shard_map/act/pallas_call | solution.py:235
  52.5 23.3 %back.1 = (bf16[16,3072]{1,0:T(8,128)(2,1)S(1)}, bf16[16,3072]{1,0:T(8,128)(2,1)S(1)}, bf16[16,3072]{1,0:T(8,128)(2,1)S(1)}, bf16[16,3072]{1,0:T(8,128)(2,1)S(1)}) custom-call(bf16[16,3072]{1,0:T(8,128)(2,1)S(1)} %get-tuple-element.35.refs_0_, bf16[16,3072]{1,0:T(8,128)(2,1)S(1)} %collective-permute-done.6.refs_1_, ...), custom_call_target="tpu_custom_call" | custom-call | tf_op jit(solution)/shard_map/back/pallas_call | solution.py:235
  75.8 1.9 %collective-permute-start.10 = (bf16[16,3072]{1,0:T(8,128)(2,1)S(1)}, bf16[16,3072]{1,0:T(8,128)(2,1)S(1)}, u32[]{:S(2)}, u32[]{:S(2)}) collective-permute-start(bf16[16,3072]{1,0:T(8,128)(2,1)S(1)} %get-tuple-element.42), channel_id=1, source_target_pairs={{8,2},{9,3},{10,0},{11,1},{12,6},{13,7},{14,4},{15,5},{16,10},{17,... | collective-permute-start | bytes 294920 | tf_op jit(solution)/shard_map/ppermute | solution.py:254
  77.8 1.9 %collective-permute-start.11 = (bf16[16,3072]{1,0:T(8,128)(2,1)S(1)}, bf16[16,3072]{1,0:T(8,128)(2,1)S(1)}, u32[]{:S(2)}, u32[]{:S(2)}) collective-permute-start(bf16[16,3072]{1,0:T(8,128)(2,1)S(1)} %get-tuple-element.43), channel_id=1, source_target_pairs={{8,1},{9,0},{10,3},{11,2},{12,5},{13,4},{14,7},{15,6},{16,9},{17,8... | collective-permute-start | bytes 294920 | tf_op jit(solution)/shard_map/ppermute | solution.py:254
  79.7 1.9 %collective-permute-start.12 = (bf16[16,3072]{1,0:T(8,128)(2,1)S(1)}, bf16[16,3072]{1,0:T(8,128)(2,1)S(1)}, u32[]{:S(2)}, u32[]{:S(2)}) collective-permute-start(bf16[16,3072]{1,0:T(8,128)(2,1)S(1)} %get-tuple-element.44), channel_id=1, source_target_pairs={{8,0},{9,1},{10,2},{11,3},{12,4},{13,5},{14,6},{15,7},{16,8},{17,9... | collective-permute-start | bytes 294920 | tf_op jit(solution)/shard_map/ppermute | solution.py:254
  81.6 1.9 %collective-permute-start.9 = (bf16[16,3072]{1,0:T(8,128)(2,1)S(1)}, bf16[16,3072]{1,0:T(8,128)(2,1)S(1)}, u32[]{:S(2)}, u32[]{:S(2)}) collective-permute-start(bf16[16,3072]{1,0:T(8,128)(2,1)S(1)} %get-tuple-element.41), channel_id=1, source_target_pairs={{8,3},{9,2},{10,1},{11,0},{12,7},{13,6},{14,5},{15,4},{16,11},{17,... | collective-permute-start | bytes 294920 | tf_op jit(solution)/shard_map/ppermute | solution.py:254
  83.6 3.5 %collective-permute-done.10.refs_1_ = bf16[16,3072]{1,0:T(8,128)(2,1)S(1)} collective-permute-done((bf16[16,3072]{1,0:T(8,128)(2,1)S(1)}, bf16[16,3072]{1,0:T(8,128)(2,1)S(1)}, u32[]{:S(2)}, u32[]{:S(2)}) %collective-permute-start.10) | collective-permute-done | bytes 98336 | tf_op jit(solution)/shard_map/ppermute | solution.py:254
  87.5 4.0 %collective-permute-done.9.refs_0_ = bf16[16,3072]{1,0:T(8,128)(2,1)S(1)} collective-permute-done((bf16[16,3072]{1,0:T(8,128)(2,1)S(1)}, bf16[16,3072]{1,0:T(8,128)(2,1)S(1)}, u32[]{:S(2)}, u32[]{:S(2)}) %collective-permute-start.9) | collective-permute-done | bytes 98336 | tf_op jit(solution)/shard_map/ppermute | solution.py:254
  91.5 1.3 %collective-permute-start.13 = (f32[8,3072]{1,0:T(8,128)S(1)}, f32[8,3072]{1,0:T(8,128)S(1)}, u32[]{:S(2)}, u32[]{:S(2)}) collective-permute-start(f32[8,3072]{1,0:T(8,128)S(1)} %get-tuple-element.46), channel_id=1, source_target_pairs={{0,4},{1,5},{2,6},{3,7},{4,0},{5,1},{6,2},{7,3},{8,12},{9,13},{10,... | collective-permute-start | bytes 294920 | tf_op jit(solution)/shard_map/ppermute | solution.py:254
  92.8 2.3 %collective-permute-done.13.received = f32[8,3072]{1,0:T(8,128)S(1)} collective-permute-done((f32[8,3072]{1,0:T(8,128)S(1)}, f32[8,3072]{1,0:T(8,128)S(1)}, u32[]{:S(2)}, u32[]{:S(2)}) %collective-permute-start.13) | collective-permute-done | bytes 98336 | tf_op jit(solution)/shard_map/ppermute | solution.py:254
  95.1 3.4 %place.1 = bf16[128,3072]{1,0:T(8,128)(2,1)} custom-call(s32[1]{0:T(128)} %bitcast.own, bf16[128,3072]{1,0:T(8,128)(2,1)S(1)} %collective-permute-done.base, s32[2,128]{1,0:T(2,128)S(1)} %collective-permute-done.5.picks, f32[8,3072]{1,0:T(8,128)S(1)} %get-tuple-element.45.kept, f32[8,3072]{1,0:T(8,128)S(1)} %collective-permute-done.13.received), custom_call_target="tpu_custom_call" | custom-call | tf_op jit(solution)/shard_map/place/pallas_call | solution.py:235
  (11 shorter events, 0.6 us)
Async XLA Ops:
  1.9 93.2 %collective-permute-start = (bf16[128,3072]{1,0:T(8,128)(2,1)}, bf16[128,3072]{1,0:T(8,128)(2,1)S(1)}, u32[]{:S(2)}, u32[]{:S(2)}) collective-permute-start(bf16[128,3072]{1,0:T(8,128)(2,1)} %bitcast.18), channel_id=1, source_target_pairs={{8,0},{9,1},{10,2},{11,3},{12,4},{13,5},{14,6},{15,7},{16,8},{17,9... | collective-permute-start | bytes 2359304 | tf_op jit(solution)/shard_map/ppermute | solution.py:254
  3.9 6.6 %collective-permute-start.1 = (bf16[2,8,3072]{2,1,0:T(8,128)(2,1)S(1)}, bf16[2,8,3072]{2,1,0:T(8,128)(2,1)S(1)}, u32[]{:S(2)}, u32[]{:S(2)}) collective-permute-start(bf16[2,8,3072]{2,1,0:T(8,128)(2,1)S(1)} %get-tuple-element.30), channel_id=1, source_target_pairs={{8,12},{9,13},{10,14},{11,15},{12,8},{13,9},{14,10},{15,11},{16,20... | collective-permute-start | bytes 294920 | tf_op jit(solution)/shard_map/ppermute | solution.py:254
  10.5 17.5 %collective-permute-start.2 = (bf16[16,3072]{1,0:T(8,128)(2,1)S(1)}, bf16[16,3072]{1,0:T(8,128)(2,1)S(1)}, u32[]{:S(2)}, u32[]{:S(2)}) collective-permute-start(bf16[16,3072]{1,0:T(8,128)(2,1)S(1)} %get-tuple-element.36.refs_0_), channel_id=1, source_target_pairs={{8,11},{9,10},{10,9},{11,8},{12,15},{13,14},{14,13},{15,12},{16,19... | collective-permute-start | bytes 294920 | tf_op jit(solution)/shard_map/ppermute | solution.py:254
  15.9 15.0 %collective-permute-start.3 = (bf16[16,3072]{1,0:T(8,128)(2,1)S(1)}, bf16[16,3072]{1,0:T(8,128)(2,1)S(1)}, u32[]{:S(2)}, u32[]{:S(2)}) collective-permute-start(bf16[16,3072]{1,0:T(8,128)(2,1)S(1)} %get-tuple-element.36.refs_0_), channel_id=1, source_target_pairs={{8,10},{9,11},{10,8},{11,9},{12,14},{13,15},{14,12},{15,13},{16,18... | collective-permute-start | bytes 294920 | tf_op jit(solution)/shard_map/ppermute | solution.py:254
  17.9 6.6 %collective-permute-start.5 = (s32[2,128]{1,0:T(2,128)}, s32[2,128]{1,0:T(2,128)S(1)}, u32[]{:S(2)}, u32[]{:S(2)}) collective-permute-start(s32[2,128]{1,0:T(2,128)} %bitcast.21), channel_id=1, source_target_pairs={{8,0},{9,1},{10,2},{11,3},{12,4},{13,5},{14,6},{15,7},{16,8},{17,9... | collective-permute-start | bytes 3080 | tf_op jit(solution)/shard_map/ppermute | solution.py:254
  19.8 22.1 %collective-permute-start.4 = (bf16[16,3072]{1,0:T(8,128)(2,1)S(1)}, bf16[16,3072]{1,0:T(8,128)(2,1)S(1)}, u32[]{:S(2)}, u32[]{:S(2)}) collective-permute-start(bf16[16,3072]{1,0:T(8,128)(2,1)S(1)} %get-tuple-element.36.refs_0_), channel_id=1, source_target_pairs={{8,9},{9,8},{10,11},{11,10},{12,13},{13,12},{14,15},{15,14},{16,17... | collective-permute-start | bytes 294920 | tf_op jit(solution)/shard_map/ppermute | solution.py:254
  24.4 28.0 %collective-permute-start.6 = (bf16[16,3072]{1,0:T(8,128)(2,1)S(1)}, bf16[16,3072]{1,0:T(8,128)(2,1)S(1)}, u32[]{:S(2)}, u32[]{:S(2)}) collective-permute-start(bf16[16,3072]{1,0:T(8,128)(2,1)S(1)} %get-tuple-element.35.refs_0_), channel_id=1, source_target_pairs={{8,11},{9,10},{10,9},{11,8},{12,15},{13,14},{14,13},{15,12},{16,19... | collective-permute-start | bytes 294920 | tf_op jit(solution)/shard_map/ppermute | solution.py:254
  28.0 24.5 %collective-permute-start.7 = (bf16[16,3072]{1,0:T(8,128)(2,1)S(1)}, bf16[16,3072]{1,0:T(8,128)(2,1)S(1)}, u32[]{:S(2)}, u32[]{:S(2)}) collective-permute-start(bf16[16,3072]{1,0:T(8,128)(2,1)S(1)} %get-tuple-element.35.refs_0_), channel_id=1, source_target_pairs={{8,10},{9,11},{10,8},{11,9},{12,14},{13,15},{14,12},{15,13},{16,18... | collective-permute-start | bytes 294920 | tf_op jit(solution)/shard_map/ppermute | solution.py:254
  30.9 21.6 %collective-permute-start.8 = (bf16[16,3072]{1,0:T(8,128)(2,1)S(1)}, bf16[16,3072]{1,0:T(8,128)(2,1)S(1)}, u32[]{:S(2)}, u32[]{:S(2)}) collective-permute-start(bf16[16,3072]{1,0:T(8,128)(2,1)S(1)} %get-tuple-element.35.refs_0_), channel_id=1, source_target_pairs={{8,9},{9,8},{10,11},{11,10},{12,13},{13,12},{14,15},{15,14},{16,17... | collective-permute-start | bytes 294920 | tf_op jit(solution)/shard_map/ppermute | solution.py:254
  75.8 11.2 %collective-permute-start.10 = (bf16[16,3072]{1,0:T(8,128)(2,1)S(1)}, bf16[16,3072]{1,0:T(8,128)(2,1)S(1)}, u32[]{:S(2)}, u32[]{:S(2)}) collective-permute-start(bf16[16,3072]{1,0:T(8,128)(2,1)S(1)} %get-tuple-element.42), channel_id=1, source_target_pairs={{8,2},{9,3},{10,0},{11,1},{12,6},{13,7},{14,4},{15,5},{16,10},{17,... | collective-permute-start | bytes 294920 | tf_op jit(solution)/shard_map/ppermute | solution.py:254
  77.8 9.2 %collective-permute-start.11 = (bf16[16,3072]{1,0:T(8,128)(2,1)S(1)}, bf16[16,3072]{1,0:T(8,128)(2,1)S(1)}, u32[]{:S(2)}, u32[]{:S(2)}) collective-permute-start(bf16[16,3072]{1,0:T(8,128)(2,1)S(1)} %get-tuple-element.43), channel_id=1, source_target_pairs={{8,1},{9,0},{10,3},{11,2},{12,5},{13,4},{14,7},{15,6},{16,9},{17,8... | collective-permute-start | bytes 294920 | tf_op jit(solution)/shard_map/ppermute | solution.py:254
  79.7 7.8 %collective-permute-start.12 = (bf16[16,3072]{1,0:T(8,128)(2,1)S(1)}, bf16[16,3072]{1,0:T(8,128)(2,1)S(1)}, u32[]{:S(2)}, u32[]{:S(2)}) collective-permute-start(bf16[16,3072]{1,0:T(8,128)(2,1)S(1)} %get-tuple-element.44), channel_id=1, source_target_pairs={{8,0},{9,1},{10,2},{11,3},{12,4},{13,5},{14,6},{15,7},{16,8},{17,9... | collective-permute-start | bytes 294920 | tf_op jit(solution)/shard_map/ppermute | solution.py:254
  81.6 9.8 %collective-permute-start.9 = (bf16[16,3072]{1,0:T(8,128)(2,1)S(1)}, bf16[16,3072]{1,0:T(8,128)(2,1)S(1)}, u32[]{:S(2)}, u32[]{:S(2)}) collective-permute-start(bf16[16,3072]{1,0:T(8,128)(2,1)S(1)} %get-tuple-element.41), channel_id=1, source_target_pairs={{8,3},{9,2},{10,1},{11,0},{12,7},{13,6},{14,5},{15,4},{16,11},{17,... | collective-permute-start | bytes 294920 | tf_op jit(solution)/shard_map/ppermute | solution.py:254
  91.5 3.5 %collective-permute-start.13 = (f32[8,3072]{1,0:T(8,128)S(1)}, f32[8,3072]{1,0:T(8,128)S(1)}, u32[]{:S(2)}, u32[]{:S(2)}) collective-permute-start(f32[8,3072]{1,0:T(8,128)S(1)} %get-tuple-element.46), channel_id=1, source_target_pairs={{0,4},{1,5},{2,6},{3,7},{4,0},{5,1},{6,2},{7,3},{8,12},{9,13},{10,... | collective-permute-start | bytes 294920 | tf_op jit(solution)/shard_map/ppermute | solution.py:254

commit v3 on v2

--- a/solution.py
+++ b/solution.py
@@ -51,7 +51,7 @@
     table = jnp.concatenate(tables, axis=0).astype(BF16)
     sent_in = dot(table, tokens, NN).astype(BF16)
     sent_grad = (jnp.concatenate(weights, axis=0) * dot(table, upstream, NN)).astype(BF16)
-    return sent_in, sent_grad
+    return sent_in, sent_grad, table
 
 
 def load(sources, targets, sems):
@@ -66,19 +66,28 @@
     return [target[...] for target in targets]
 
 
-def route_body(own, picks, pick_weights, tokens, grad_out, kept_in, kept_grad, sent, *scratch):
+def fill(ahead, upstream, table):
+    count = upstream.shape[0]
+    ahead[:count, :] = upstream
+    ahead[count:, :] = jnp.zeros((EF * CAP, ahead.shape[1]), BF16)
+    ahead[count:, :count] = table
+
+
+def route_body(own, picks, pick_weights, tokens, grad_out, kept_in, kept_grad, sent, ahead, *scratch):
     loaded = load((picks, pick_weights, tokens, grad_out), scratch[:-1], scratch[-1])
     first = own[0]
-    rows_in, rows_grad = select((first, 1 - first), *loaded)
+    rows_in, rows_grad, table = select((first, 1 - first), *loaded)
     kept_in[...] = rows_in[:CAP]
     kept_grad[...] = rows_grad[:CAP]
     sent[0] = rows_grad[CAP:]
     sent[1] = rows_in[CAP:]
-
-
-def route_all_body(picks, pick_weights, tokens, grad_out, rows_in, rows_grad, *scratch):
+    fill(ahead, loaded[3], table)
+
+
+def route_all_body(picks, pick_weights, tokens, grad_out, rows_in, rows_grad, ahead, *scratch):
     loaded = load((picks, pick_weights, tokens, grad_out), scratch[:-1], scratch[-1])
-    sent_in, sent_grad = select(range(EF), *loaded)
+    sent_in, sent_grad, table = select(range(EF), *loaded)
+    fill(ahead, loaded[3], table)
     group = rows_in.shape[0] // EF
     for expert in range(EF):
         for member in range(group):
@@ -86,9 +95,11 @@
             rows_grad[expert * group + member] = sent_grad[expert * CAP : (expert + 1) * CAP]
 
 
-def join_body(kept_in, kept_grad, received, rows_in, rows_grad):
+def join_body(kept_in, kept_grad, received, rows_in, rows_grad, both):
     rows_in[...] = jnp.concatenate([kept_in[...], received[1]], axis=0)
     rows_grad[...] = jnp.concatenate([kept_grad[...], received[0]], axis=0)
+    both[0] = rows_grad[...]
+    both[1] = rows_in[...]
 
 
 def act_body(*refs, pieces, block):
@@ -103,7 +114,7 @@
 
     for index in range(min(depth, count)):
         fetch(index).start()
-    gather(refs[:pieces], rows)
+    gather(refs[:pieces], rows, 0)
     for index in range(count):
         fetch(index).wait()
         act_grad[:, pl.ds(index * block, block)] = dot(rows[...], buffers[index % depth], NT)
@@ -111,9 +122,11 @@
             fetch(index + depth).start()
 
 
-def gather(pieces, rows):
+def gather(pieces, rows, which):
     start = 0
     for piece in pieces:
+        if len(piece.shape) > 2:
+            piece = piece.at[which]
         size = piece.shape[0]
         rows[pl.ds(start, size), :] = piece[...]
         start += size
@@ -121,7 +134,7 @@
         rows[pl.ds(start, rows.shape[0] - start), :] = jnp.zeros((rows.shape[0] - start, rows.shape[1]), BF16)
 
 
-def back_body(*refs, pieces, block, chunk, kept):
+def back_body(*refs, pieces, block, chunk):
     act_grad, gate, up = refs[pieces : pieces + 3]
     outs = refs[pieces + 3 : 2 * pieces + 3]
     rows_in, total, *buffers, sems = refs[2 * pieces + 3 :]
@@ -130,29 +143,25 @@
     width, hidden = gate.shape
     count = hidden // block
     depth = buffers[0].shape[0]
-    sources = ((up,) if kept else (up, gate))
 
     def fetch(index):
         slot = index % depth
         part = pl.ds(index * block, block)
         return [
             pltpu.make_async_copy(source.at[:, part], buffer.at[slot], sems.at[order, slot])
-            for order, (source, buffer) in enumerate(zip(sources, buffers))
+            for order, (source, buffer) in enumerate(zip((up, gate), buffers))
         ]
 
     for index in range(min(depth, count)):
         for copy in reversed(fetch(index)):
             copy.start()
-    gather(refs[:pieces], rows_in)
+    gather(refs[:pieces], rows_in, 1)
     for index in range(count):
         part = pl.ds(index * block, block)
         slot = index % depth
         copies = fetch(index)
-        if kept:
-            gates = gate.at[:, part]
-        else:
-            copies[1].wait()
-            gates = buffers[1].at[slot]
+        copies[1].wait()
+        gates = buffers[1].at[slot]
         ups = buffers[0].at[slot]
         gate_pre = dot(rows_in[...], gates[...], NN)[:slots]
         copies[0].wait()
@@ -195,34 +204,20 @@
         total[...] = value
 
 
-def place_body(own, base, picks, kept, received, out):
-    first = own[0]
-    table = jnp.concatenate([slot_table(picks[...], first), slot_table(picks[...], 1 - first)], axis=0)
-    total = jnp.concatenate([kept[...], received[...]], axis=0)
-    branch = lax.dot_general(table, total, TN, precision=lax.Precision.HIGHEST, preferred_element_type=F32)
-    out[...] = (base[...].astype(F32) + branch).astype(BF16)
-
-
-def hold_body(source, target, sem):
-    copy = pltpu.make_async_copy(source, target, sem)
-    copy.start()
-    copy.wait()
-
-
-def hold(value):
-    return call(
-        hold_body,
-        pltpu.VMEM(value.shape, value.dtype),
-        (value,),
-        [HBM],
-        "hold",
-        1 * MIB,
-        scratch_shapes=[pltpu.SemaphoreType.DMA],
-    )
-
-
-def resident(value):
-    return pltpu.with_memory_space_constraint(value, pltpu.VMEM)
+def place_body(ahead, kept, received, out, done, sems):
+    count, width = out.shape
+    table = ahead[count:, :count].astype(F32)
+    chunk = width // sems.shape[0]
+    copies = []
+    for index in range(sems.shape[0]):
+        part = pl.ds(index * chunk, chunk)
+        total = jnp.concatenate([kept[:, part], received[:, part]], axis=0)
+        branch = lax.dot_general(table, total, TN, precision=lax.Precision.HIGHEST, preferred_element_type=F32)
+        done[:, part] = (ahead[:count, part].astype(F32) + branch).astype(BF16)
+        copies.append(pltpu.make_async_copy(done.at[:, part], out.at[:, part], sems.at[index]))
+        copies[-1].start()
+    for copy in copies:
+        copy.wait()
 
 
 def call(body, out_shape, args, in_specs, name, limit, **kwargs):
@@ -277,38 +272,43 @@
     sources = (picks, pick_weights, inputs, upstream)
     staging = [pltpu.VMEM(source.shape, source.dtype) for source in sources] + [pltpu.SemaphoreType.DMA((4,))]
 
+    ahead_shape = shape((count + EF * CAP, width), BF16)
     if paired:
         eight = shape((CAP, width), BF16)
-        kept_in, kept_grad, sent = call(
+        kept_in, kept_grad, sent, ahead = call(
             route_body,
-            [eight, eight, shape((2, CAP, width), BF16)],
+            [eight, eight, shape((2, CAP, width), BF16), ahead_shape],
             (own, *sources),
             [SMEM] + [HBM] * 4,
             "route",
             16 * MIB,
             scratch_shapes=staging,
         )
-        sent, picks, upstream = lax.optimization_barrier((sent, picks, upstream))
         received = send(sent, lambda p, e, d: (p, 1 - e, d))
-        next_upstream = to_previous(upstream)
-        next_picks = to_previous(picks)
+        ahead, received = lax.optimization_barrier((ahead, received))
         sixteen = shape((EF * CAP, width), BF16)
-        near_in, near_grad = call(
-            join_body, [sixteen, sixteen], (kept_in, kept_grad, received), [VMEM] * 3, "join", 8 * MIB
+        near_in, near_grad, near_both = call(
+            join_body,
+            [sixteen, sixteen, shape((2, EF * CAP, width), BF16)],
+            (kept_in, kept_grad, received),
+            [VMEM] * 3,
+            "join",
+            8 * MIB,
         )
-        order = [step for step in reversed(range(1, lines))]
+        order = [step for step in reversed(range(2, lines))]
         far_grad = [send(near_grad, lambda p, e, d, step=step: (p, e, d ^ step)) for step in order]
+        both = send(near_both, lambda p, e, d: (p, e, d ^ 1))
         far_in = [send(near_in, lambda p, e, d, step=step: (p, e, d ^ step)) for step in order]
-        grad_pieces = [near_grad] + far_grad
-        in_pieces = [near_in] + far_in
-        near_grad, gate = lax.optimization_barrier((near_grad, gate))
-        gate = hold(gate)
-        grad_pieces, next_picks, gate = lax.optimization_barrier((grad_pieces, next_picks, gate))
+        ahead = to_previous(ahead)
+        order = order + [1, 0]
+        grad_pieces = far_grad + [both, near_grad]
+        in_pieces = far_in + [both, near_in]
+        grad_pieces, ahead = lax.optimization_barrier((grad_pieces, ahead))
     else:
         bound = shape((members, CAP, width), BF16)
-        sent_in, sent_grad = call(
+        sent_in, sent_grad, ahead = call(
             route_all_body,
-            [bound, bound],
+            [bound, bound, ahead_shape],
             sources,
             [HBM] * 4,
             "route",
@@ -317,8 +317,7 @@
         )
         grad_pieces = [exchange(sent_grad).reshape(slots, width)]
         in_pieces = [exchange(sent_in).reshape(slots, width)]
-        next_upstream = to_previous(upstream)
-        next_picks = to_previous(picks)
+        ahead = to_previous(ahead)
 
     pieces = len(in_pieces)
     block = min(hidden, 512)
@@ -338,24 +337,23 @@
     )
     depth = 3
     partial = call(
-        functools.partial(back_body, pieces=pieces, block=block, chunk=512, kept=paired),
+        functools.partial(back_body, pieces=pieces, block=block, chunk=512),
         [shape((slots // pieces, width), BF16)] * pieces,
-        (*in_pieces, act_grad, resident(gate) if paired else gate, up),
-        [VMEM] * (pieces + 1) + [VMEM if paired else HBM, HBM],
+        (*in_pieces, act_grad, gate, up),
+        [VMEM] * (pieces + 1) + [HBM, HBM],
         "back",
-        (20 if paired else 40) * MIB,
+        40 * MIB,
         scratch_shapes=[
             pltpu.VMEM((max(128, slots), width), BF16),
             pltpu.VMEM((width, slots), F32),
-            *[pltpu.VMEM((depth, width, block), BF16)] * (1 if paired else 2),
+            pltpu.VMEM((depth, width, block), BF16),
+            pltpu.VMEM((depth, width, block), BF16),
             pltpu.SemaphoreType.DMA((2, depth)),
         ],
     )
     total = shape((CAP, width), F32)
     if paired:
-        steps = order + [0]
-        given = partial[1:] + partial[:1]
-        parts = [send(part, lambda p, e, d, step=step: (p - 1, e, d ^ step)) for part, step in zip(given, steps)]
+        parts = [send(part, lambda p, e, d, step=step: (p - 1, e, d ^ step)) for part, step in zip(partial, order)]
         kept, sent = call(sum_body, [total, total], parts, [VMEM] * pieces, "sum", 16 * MIB)
         received = send(sent, lambda p, e, d: (p, 1 - e, d), first=0)
     else:
@@ -363,22 +361,15 @@
         kept, received = map(
             to_previous, call(sum_all_body, [total, total], (returned,), [VMEM], "sum", 16 * MIB)
         )
-    columns = 768
     out = call(
         place_body,
         shape((count, width), BF16),
-        (own, next_upstream, next_picks, kept, received),
-        [
-            SMEM,
-            pl.BlockSpec((count, columns), lambda i: (0, i)),
-            pl.BlockSpec(picks.shape, lambda i: (0, 0)),
-            pl.BlockSpec((CAP, columns), lambda i: (0, i)),
-            pl.BlockSpec((CAP, columns), lambda i: (0, i)),
-        ],
+        (ahead, kept, received),
+        [VMEM] * 3,
         "place",
-        16 * MIB,
-        grid=(width // columns,),
-        out_specs=pl.BlockSpec((count, columns), lambda i: (0, i)),
+        8 * MIB,
+        out_specs=HBM,
+        scratch_shapes=[pltpu.VMEM((count, width), BF16), pltpu.SemaphoreType.DMA((4,))],
     )
     return out[None]
 

time: 99 us -> 87.6 us (0.88)
  Pallas kernels: 47.4 us -> 39.7 us
  starting transfers between devices: 36.3 us -> 31.5 us
  waiting for transfers between devices: 14.6 us -> 15.7 us
    pallas_call x7 -> x6, Pallas kernels: 47.4 us -> 39.7 us  [call(): pl.pallas_call(body, out_shape=out_shape, in_specs=in_specs, out_specs=kw...]
    ppermute x14 -> x12, starting transfers between devices: 36.3 us -> 31.5 us  [send(): return lax.ppermute(value, AXES, pairs)]
    ppermute x14 -> x12, waiting for transfers between devices: 14.6 us -> 15.7 us  [send(): return lax.ppermute(value, AXES, pairs)]
  transfers between devices with their start and end apart: 14 -> 12, of which waited for: 6 -> 5; matrix products, arithmetic and copies ran while one was open for 0% -> 0% of each run, Pallas kernels for 43% -> 12%
where the time goes in v3:
time: 87.6 us; the launch traced here: 87.2 us
  Pallas kernels  39.7 us (45%)
  starting transfers between devices  31.5 us (36%)
  waiting for transfers between devices  15.7 us (18%)
    pallas_call x6, Pallas kernels, call(): pl.pallas_call(body, out_shape=out_shape, in_specs=in_specs, out_specs=kw...  39.7 us
    ppermute x12, starting transfers between devices, send(): return lax.ppermute(value, AXES, pairs)  31.5 us
    ppermute x12, waiting for transfers between devices, send(): return lax.ppermute(value, AXES, pairs)  15.7 us
  transfers between devices with their start and end apart: 12, of which 5 were waited for; matrix products, arithmetic and copies ran while one was open for 0% of the time, Pallas kernels for 12%

profile of v3, /device:TPU:1, one launch (start us, length us, event | category | flops | bytes accessed | tf_op | source)
XLA Modules:
  0.0 87.2 jit_solution(16793797726353070040)
XLA Ops:
  0.0 1.9 %route.1 = (bf16[8,3072]{1,0:T(8,128)(2,1)S(1)}, bf16[8,3072]{1,0:T(8,128)(2,1)S(1)}, bf16[2,8,3072]{2,1,0:T(8,128)(2,1)S(1)}, bf16[144,3072]{1,0:T(8,128)(2,1)S(1)}) custom-call(s32[1]{0:T(128)} %bitcast.own, s32[2,128]{1,0:T(2,128)} %bitcast.18, f32[2,128]{1,0:T(2,128)} %bitcast.19, bf16[128,3072]{1,0:T(8,128)(2,1)} %bitcast.16, bf16[128,3072]{1,0:T(8,128)(2,1)} %bitcast.17), custom_call_target="tpu_custom_call" | custom-call | tf_op jit(solution)/shard_map/route/pallas_call | solution.py:230
  1.9 3.9 %collective-permute-start = (bf16[2,8,3072]{2,1,0:T(8,128)(2,1)S(1)}, bf16[2,8,3072]{2,1,0:T(8,128)(2,1)S(1)}, u32[]{:S(2)}, u32[]{:S(2)}) collective-permute-start(bf16[2,8,3072]{2,1,0:T(8,128)(2,1)S(1)} %get-tuple-element.28), channel_id=1, source_target_pairs={{8,12},{9,13},{10,14},{11,15},{12,8},{13,9},{14,10},{15,11},{16,20... | collective-permute-start | bytes 294920 | tf_op jit(solution)/shard_map/ppermute | solution.py:249
  5.8 2.0 %collective-permute-done.received = bf16[2,8,3072]{2,1,0:T(8,128)(2,1)S(1)} collective-permute-done((bf16[2,8,3072]{2,1,0:T(8,128)(2,1)S(1)}, bf16[2,8,3072]{2,1,0:T(8,128)(2,1)S(1)}, u32[]{:S(2)}, u32[]{:S(2)}) %collective-permute-start) | collective-permute-done | bytes 98336 | tf_op jit(solution)/shard_map/ppermute | solution.py:249
  7.8 1.9 %collective-permute-start.4 = (bf16[144,3072]{1,0:T(8,128)(2,1)S(1)}, bf16[144,3072]{1,0:T(8,128)(2,1)S(1)}, u32[]{:S(2)}, u32[]{:S(2)}) collective-permute-start(bf16[144,3072]{1,0:T(8,128)(2,1)S(1)} %get-tuple-element.32), channel_id=1, source_target_pairs={{8,0},{9,1},{10,2},{11,3},{12,4},{13,5},{14,6},{15,7},{16,8},{17,9... | collective-permute-start | bytes 2654216 | tf_op jit(solution)/shard_map/ppermute | solution.py:249
  9.8 3.4 %collective-permute-start.3 = (bf16[2,16,3072]{2,1,0:T(8,128)(2,1)S(1)}, bf16[2,16,3072]{2,1,0:T(8,128)(2,1)S(1)}, u32[]{:S(2)}, u32[]{:S(2)}) collective-permute-start(bf16[2,16,3072]{2,1,0:T(8,128)(2,1)S(1)} %get-tuple-element.31), channel_id=1, source_target_pairs={{8,9},{9,8},{10,11},{11,10},{12,13},{13,12},{14,15},{15,14},{16,17... | collective-permute-start | bytes 589832 | tf_op jit(solution)/shard_map/ppermute | solution.py:249
  13.3 4.2 %collective-permute-start.2 = (bf16[16,3072]{1,0:T(8,128)(2,1)S(1)}, bf16[16,3072]{1,0:T(8,128)(2,1)S(1)}, u32[]{:S(2)}, u32[]{:S(2)}) collective-permute-start(bf16[16,3072]{1,0:T(8,128)(2,1)S(1)} %get-tuple-element.38.refs_3_), channel_id=1, source_target_pairs={{8,10},{9,11},{10,8},{11,9},{12,14},{13,15},{14,12},{15,13},{16,18... | collective-permute-start | bytes 294920 | tf_op jit(solution)/shard_map/ppermute | solution.py:249
  17.5 1.9 %collective-permute-start.1 = (bf16[16,3072]{1,0:T(8,128)(2,1)S(1)}, bf16[16,3072]{1,0:T(8,128)(2,1)S(1)}, u32[]{:S(2)}, u32[]{:S(2)}) collective-permute-start(bf16[16,3072]{1,0:T(8,128)(2,1)S(1)} %get-tuple-element.38.refs_3_), channel_id=1, source_target_pairs={{8,11},{9,10},{10,9},{11,8},{12,15},{13,14},{14,13},{15,12},{16,19... | collective-permute-start | bytes 294920 | tf_op jit(solution)/shard_map/ppermute | solution.py:249
  19.4 3.2 %collective-permute-start.6 = (bf16[16,3072]{1,0:T(8,128)(2,1)S(1)}, bf16[16,3072]{1,0:T(8,128)(2,1)S(1)}, u32[]{:S(2)}, u32[]{:S(2)}) collective-permute-start(bf16[16,3072]{1,0:T(8,128)(2,1)S(1)} %get-tuple-element.34.refs_3_), channel_id=1, source_target_pairs={{8,10},{9,11},{10,8},{11,9},{12,14},{13,15},{14,12},{15,13},{16,18... | collective-permute-start | bytes 294920 | tf_op jit(solution)/shard_map/ppermute | solution.py:249
  22.7 0.0 collective-permute-done.2.refs_1_
  22.7 3.8 %collective-permute-start.5 = (bf16[16,3072]{1,0:T(8,128)(2,1)S(1)}, bf16[16,3072]{1,0:T(8,128)(2,1)S(1)}, u32[]{:S(2)}, u32[]{:S(2)}) collective-permute-start(bf16[16,3072]{1,0:T(8,128)(2,1)S(1)} %get-tuple-element.34.refs_3_), channel_id=1, source_target_pairs={{8,11},{9,10},{10,9},{11,8},{12,15},{13,14},{14,13},{15,12},{16,19... | collective-permute-start | bytes 294920 | tf_op jit(solution)/shard_map/ppermute | solution.py:249
  26.5 0.0 collective-permute-done.4.ahead
  26.6 10.5 %act.1.refs_4_ = f32[64,4096]{1,0:T(8,128)S(1)} custom-call(bf16[16,3072]{1,0:T(8,128)(2,1)S(1)} %collective-permute-done.1.refs_0_, bf16[16,3072]{1,0:T(8,128)(2,1)S(1)} %collective-permute-done.2.refs_1_, bf16[2,16,3072]{2,1,0:T(8,128)(2,1)S(1)} %collective-permute-done.3.refs_2_, bf16[16,3072]{1,0:T(8,128)(2,1)S(1)} %get-tuple-element.38.refs_3_, ...), custom_call_target="tpu_custom_call" | custom-call | tf_op jit(solution)/shard_map/act/pallas_call | solution.py:230
  37.1 0.0 collective-permute-done.5.refs_0_
  37.1 25.1 %back.1 = (bf16[16,3072]{1,0:T(8,128)(2,1)S(1)}, bf16[16,3072]{1,0:T(8,128)(2,1)S(1)}, bf16[16,3072]{1,0:T(8,128)(2,1)S(1)}, bf16[16,3072]{1,0:T(8,128)(2,1)S(1)}) custom-call(bf16[16,3072]{1,0:T(8,128)(2,1)S(1)} %collective-permute-done.5.refs_0_, bf16[16,3072]{1,0:T(8,128)(2,1)S(1)} %collective-permute-done.6.refs_1_, ...), custom_call_target="tpu_custom_call" | custom-call | tf_op jit(solution)/shard_map/back/pallas_call | solution.py:230
  62.2 1.9 %collective-permute-start.7 = (bf16[16,3072]{1,0:T(8,128)(2,1)S(1)}, bf16[16,3072]{1,0:T(8,128)(2,1)S(1)}, u32[]{:S(2)}, u32[]{:S(2)}) collective-permute-start(bf16[16,3072]{1,0:T(8,128)(2,1)S(1)} %get-tuple-element.39), channel_id=1, source_target_pairs={{8,3},{9,2},{10,1},{11,0},{12,7},{13,6},{14,5},{15,4},{16,11},{17,... | collective-permute-start | bytes 294920 | tf_op jit(solution)/shard_map/ppermute | solution.py:249
  64.1 1.9 %collective-permute-start.8 = (bf16[16,3072]{1,0:T(8,128)(2,1)S(1)}, bf16[16,3072]{1,0:T(8,128)(2,1)S(1)}, u32[]{:S(2)}, u32[]{:S(2)}) collective-permute-start(bf16[16,3072]{1,0:T(8,128)(2,1)S(1)} %get-tuple-element.40), channel_id=1, source_target_pairs={{8,2},{9,3},{10,0},{11,1},{12,6},{13,7},{14,4},{15,5},{16,10},{17,... | collective-permute-start | bytes 294920 | tf_op jit(solution)/shard_map/ppermute | solution.py:249
  66.1 1.9 %collective-permute-start.9 = (bf16[16,3072]{1,0:T(8,128)(2,1)S(1)}, bf16[16,3072]{1,0:T(8,128)(2,1)S(1)}, u32[]{:S(2)}, u32[]{:S(2)}) collective-permute-start(bf16[16,3072]{1,0:T(8,128)(2,1)S(1)} %get-tuple-element.41), channel_id=1, source_target_pairs={{8,1},{9,0},{10,3},{11,2},{12,5},{13,4},{14,7},{15,6},{16,9},{17,8... | collective-permute-start | bytes 294920 | tf_op jit(solution)/shard_map/ppermute | solution.py:249
  68.0 1.9 %collective-permute-start.10 = (bf16[16,3072]{1,0:T(8,128)(2,1)S(1)}, bf16[16,3072]{1,0:T(8,128)(2,1)S(1)}, u32[]{:S(2)}, u32[]{:S(2)}) collective-permute-start(bf16[16,3072]{1,0:T(8,128)(2,1)S(1)} %get-tuple-element.42), channel_id=1, source_target_pairs={{8,0},{9,1},{10,2},{11,3},{12,4},{13,5},{14,6},{15,7},{16,8},{17,9... | collective-permute-start | bytes 294920 | tf_op jit(solution)/shard_map/ppermute | solution.py:249
  69.9 5.2 %collective-permute-done.7.refs_0_ = bf16[16,3072]{1,0:T(8,128)(2,1)S(1)} collective-permute-done((bf16[16,3072]{1,0:T(8,128)(2,1)S(1)}, bf16[16,3072]{1,0:T(8,128)(2,1)S(1)}, u32[]{:S(2)}, u32[]{:S(2)}) %collective-permute-start.7) | collective-permute-done | bytes 98336 | tf_op jit(solution)/shard_map/ppermute | solution.py:249
  75.1 4.4 %collective-permute-done.8.refs_1_ = bf16[16,3072]{1,0:T(8,128)(2,1)S(1)} collective-permute-done((bf16[16,3072]{1,0:T(8,128)(2,1)S(1)}, bf16[16,3072]{1,0:T(8,128)(2,1)S(1)}, u32[]{:S(2)}, u32[]{:S(2)}) %collective-permute-start.8) | collective-permute-done | bytes 98336 | tf_op jit(solution)/shard_map/ppermute | solution.py:249
  79.5 1.9 %collective-permute-done.10.refs_3_ = bf16[16,3072]{1,0:T(8,128)(2,1)S(1)} collective-permute-done((bf16[16,3072]{1,0:T(8,128)(2,1)S(1)}, bf16[16,3072]{1,0:T(8,128)(2,1)S(1)}, u32[]{:S(2)}, u32[]{:S(2)}) %collective-permute-start.10) | collective-permute-done | bytes 98336 | tf_op jit(solution)/shard_map/ppermute | solution.py:249
  81.4 1.3 %collective-permute-start.11 = (f32[8,3072]{1,0:T(8,128)S(1)}, f32[8,3072]{1,0:T(8,128)S(1)}, u32[]{:S(2)}, u32[]{:S(2)}) collective-permute-start(f32[8,3072]{1,0:T(8,128)S(1)} %get-tuple-element.44), channel_id=1, source_target_pairs={{0,4},{1,5},{2,6},{3,7},{4,0},{5,1},{6,2},{7,3},{8,12},{9,13},{10,... | collective-permute-start | bytes 294920 | tf_op jit(solution)/shard_map/ppermute | solution.py:249
  82.6 2.3 %collective-permute-done.11.received = f32[8,3072]{1,0:T(8,128)S(1)} collective-permute-done((f32[8,3072]{1,0:T(8,128)S(1)}, f32[8,3072]{1,0:T(8,128)S(1)}, u32[]{:S(2)}, u32[]{:S(2)}) %collective-permute-start.11) | collective-permute-done | bytes 98336 | tf_op jit(solution)/shard_map/ppermute | solution.py:249
  84.9 2.1 %place.1 = bf16[128,3072]{1,0:T(8,128)(2,1)} custom-call(bf16[144,3072]{1,0:T(8,128)(2,1)S(1)} %collective-permute-done.4.ahead, f32[8,3072]{1,0:T(8,128)S(1)} %get-tuple-element.43.kept, f32[8,3072]{1,0:T(8,128)S(1)} %collective-permute-done.11.received), custom_call_target="tpu_custom_call" | custom-call | tf_op jit(solution)/shard_map/place/pallas_call | solution.py:230
  (6 shorter events, 0.1 us)
Async XLA Ops:
  1.9 5.9 %collective-permute-start = (bf16[2,8,3072]{2,1,0:T(8,128)(2,1)S(1)}, bf16[2,8,3072]{2,1,0:T(8,128)(2,1)S(1)}, u32[]{:S(2)}, u32[]{:S(2)}) collective-permute-start(bf16[2,8,3072]{2,1,0:T(8,128)(2,1)S(1)} %get-tuple-element.28), channel_id=1, source_target_pairs={{8,12},{9,13},{10,14},{11,15},{12,8},{13,9},{14,10},{15,11},{16,20... | collective-permute-start | bytes 294920 | tf_op jit(solution)/shard_map/ppermute | solution.py:249
  7.8 18.7 %collective-permute-start.4 = (bf16[144,3072]{1,0:T(8,128)(2,1)S(1)}, bf16[144,3072]{1,0:T(8,128)(2,1)S(1)}, u32[]{:S(2)}, u32[]{:S(2)}) collective-permute-start(bf16[144,3072]{1,0:T(8,128)(2,1)S(1)} %get-tuple-element.32), channel_id=1, source_target_pairs={{8,0},{9,1},{10,2},{11,3},{12,4},{13,5},{14,6},{15,7},{16,8},{17,9... | collective-permute-start | bytes 2654216 | tf_op jit(solution)/shard_map/ppermute | solution.py:249
  9.8 16.7 %collective-permute-start.3 = (bf16[2,16,3072]{2,1,0:T(8,128)(2,1)S(1)}, bf16[2,16,3072]{2,1,0:T(8,128)(2,1)S(1)}, u32[]{:S(2)}, u32[]{:S(2)}) collective-permute-start(bf16[2,16,3072]{2,1,0:T(8,128)(2,1)S(1)} %get-tuple-element.31), channel_id=1, source_target_pairs={{8,9},{9,8},{10,11},{11,10},{12,13},{13,12},{14,15},{15,14},{16,17... | collective-permute-start | bytes 589832 | tf_op jit(solution)/shard_map/ppermute | solution.py:249
  13.3 9.4 %collective-permute-start.2 = (bf16[16,3072]{1,0:T(8,128)(2,1)S(1)}, bf16[16,3072]{1,0:T(8,128)(2,1)S(1)}, u32[]{:S(2)}, u32[]{:S(2)}) collective-permute-start(bf16[16,3072]{1,0:T(8,128)(2,1)S(1)} %get-tuple-element.38.refs_3_), channel_id=1, source_target_pairs={{8,10},{9,11},{10,8},{11,9},{12,14},{13,15},{14,12},{15,13},{16,18... | collective-permute-start | bytes 294920 | tf_op jit(solution)/shard_map/ppermute | solution.py:249
  17.5 9.0 %collective-permute-start.1 = (bf16[16,3072]{1,0:T(8,128)(2,1)S(1)}, bf16[16,3072]{1,0:T(8,128)(2,1)S(1)}, u32[]{:S(2)}, u32[]{:S(2)}) collective-permute-start(bf16[16,3072]{1,0:T(8,128)(2,1)S(1)} %get-tuple-element.38.refs_3_), channel_id=1, source_target_pairs={{8,11},{9,10},{10,9},{11,8},{12,15},{13,14},{14,13},{15,12},{16,19... | collective-permute-start | bytes 294920 | tf_op jit(solution)/shard_map/ppermute | solution.py:249
  19.4 17.7 %collective-permute-start.6 = (bf16[16,3072]{1,0:T(8,128)(2,1)S(1)}, bf16[16,3072]{1,0:T(8,128)(2,1)S(1)}, u32[]{:S(2)}, u32[]{:S(2)}) collective-permute-start(bf16[16,3072]{1,0:T(8,128)(2,1)S(1)} %get-tuple-element.34.refs_3_), channel_id=1, source_target_pairs={{8,10},{9,11},{10,8},{11,9},{12,14},{13,15},{14,12},{15,13},{16,18... | collective-permute-start | bytes 294920 | tf_op jit(solution)/shard_map/ppermute | solution.py:249
  22.7 14.4 %collective-permute-start.5 = (bf16[16,3072]{1,0:T(8,128)(2,1)S(1)}, bf16[16,3072]{1,0:T(8,128)(2,1)S(1)}, u32[]{:S(2)}, u32[]{:S(2)}) collective-permute-start(bf16[16,3072]{1,0:T(8,128)(2,1)S(1)} %get-tuple-element.34.refs_3_), channel_id=1, source_target_pairs={{8,11},{9,10},{10,9},{11,8},{12,15},{13,14},{14,13},{15,12},{16,19... | collective-permute-start | bytes 294920 | tf_op jit(solution)/shard_map/ppermute | solution.py:249
  62.2 12.9 %collective-permute-start.7 = (bf16[16,3072]{1,0:T(8,128)(2,1)S(1)}, bf16[16,3072]{1,0:T(8,128)(2,1)S(1)}, u32[]{:S(2)}, u32[]{:S(2)}) collective-permute-start(bf16[16,3072]{1,0:T(8,128)(2,1)S(1)} %get-tuple-element.39), channel_id=1, source_target_pairs={{8,3},{9,2},{10,1},{11,0},{12,7},{13,6},{14,5},{15,4},{16,11},{17,... | collective-permute-start | bytes 294920 | tf_op jit(solution)/shard_map/ppermute | solution.py:249
  64.1 15.3 %collective-permute-start.8 = (bf16[16,3072]{1,0:T(8,128)(2,1)S(1)}, bf16[16,3072]{1,0:T(8,128)(2,1)S(1)}, u32[]{:S(2)}, u32[]{:S(2)}) collective-permute-start(bf16[16,3072]{1,0:T(8,128)(2,1)S(1)} %get-tuple-element.40), channel_id=1, source_target_pairs={{8,2},{9,3},{10,0},{11,1},{12,6},{13,7},{14,4},{15,5},{16,10},{17,... | collective-permute-start | bytes 294920 | tf_op jit(solution)/shard_map/ppermute | solution.py:249
  66.1 13.4 %collective-permute-start.9 = (bf16[16,3072]{1,0:T(8,128)(2,1)S(1)}, bf16[16,3072]{1,0:T(8,128)(2,1)S(1)}, u32[]{:S(2)}, u32[]{:S(2)}) collective-permute-start(bf16[16,3072]{1,0:T(8,128)(2,1)S(1)} %get-tuple-element.41), channel_id=1, source_target_pairs={{8,1},{9,0},{10,3},{11,2},{12,5},{13,4},{14,7},{15,6},{16,9},{17,8... | collective-permute-start | bytes 294920 | tf_op jit(solution)/shard_map/ppermute | solution.py:249
  68.0 13.3 %collective-permute-start.10 = (bf16[16,3072]{1,0:T(8,128)(2,1)S(1)}, bf16[16,3072]{1,0:T(8,128)(2,1)S(1)}, u32[]{:S(2)}, u32[]{:S(2)}) collective-permute-start(bf16[16,3072]{1,0:T(8,128)(2,1)S(1)} %get-tuple-element.42), channel_id=1, source_target_pairs={{8,0},{9,1},{10,2},{11,3},{12,4},{13,5},{14,6},{15,7},{16,8},{17,9... | collective-permute-start | bytes 294920 | tf_op jit(solution)/shard_map/ppermute | solution.py:249
  81.4 3.5 %collective-permute-start.11 = (f32[8,3072]{1,0:T(8,128)S(1)}, f32[8,3072]{1,0:T(8,128)S(1)}, u32[]{:S(2)}, u32[]{:S(2)}) collective-permute-start(f32[8,3072]{1,0:T(8,128)S(1)} %get-tuple-element.44), channel_id=1, source_target_pairs={{0,4},{1,5},{2,6},{3,7},{4,0},{5,1},{6,2},{7,3},{8,12},{9,13},{10,... | collective-permute-start | bytes 294920 | tf_op jit(solution)/shard_map/ppermute | solution.py:249

commit v4 on v3

--- a/solution.py
+++ b/solution.py
@@ -103,8 +103,12 @@
 
 
 def act_body(*refs, pieces, block):
-    down, act_grad, rows, buffers, sems = refs[pieces:]
+    down, gate, up, act_grad, gate_first, up_first, rows, buffers, sems, first_sems = refs[pieces:]
     hidden = down.shape[0]
+    early = [
+        pltpu.make_async_copy(source.at[:, pl.ds(0, block)], target, first_sems.at[order])
+        for order, (source, target) in enumerate(((gate, gate_first), (up, up_first)))
+    ]
     count = hidden // block
     depth = buffers.shape[0]
 
@@ -120,6 +124,11 @@
         act_grad[:, pl.ds(index * block, block)] = dot(rows[...], buffers[index % depth], NT)
         if index + depth < count:
             fetch(index + depth).start()
+        elif index + depth == max(count, depth):
+            for copy in early:
+                copy.start()
+    for copy in early:
+        copy.wait()
 
 
 def gather(pieces, rows, which):
@@ -135,9 +144,9 @@
 
 
 def back_body(*refs, pieces, block, chunk):
-    act_grad, gate, up = refs[pieces : pieces + 3]
-    outs = refs[pieces + 3 : 2 * pieces + 3]
-    rows_in, total, *buffers, sems = refs[2 * pieces + 3 :]
+    act_grad, gate, up, gate_first, up_first = refs[pieces : pieces + 5]
+    outs = refs[pieces + 5 : 2 * pieces + 5]
+    rows_in, total, *buffers, sems = refs[2 * pieces + 5 :]
     slots = act_grad.shape[0]
     size = slots // pieces
     width, hidden = gate.shape
@@ -152,19 +161,20 @@
             for order, (source, buffer) in enumerate(zip((up, gate), buffers))
         ]
 
-    for index in range(min(depth, count)):
+    for index in range(1, min(depth + 1, count)):
         for copy in reversed(fetch(index)):
             copy.start()
     gather(refs[:pieces], rows_in, 1)
     for index in range(count):
         part = pl.ds(index * block, block)
         slot = index % depth
-        copies = fetch(index)
-        copies[1].wait()
-        gates = buffers[1].at[slot]
-        ups = buffers[0].at[slot]
+        copies = fetch(index) if index else None
+        gates, ups = (buffers[1].at[slot], buffers[0].at[slot]) if index else (gate_first, up_first)
+        if index:
+            copies[1].wait()
         gate_pre = dot(rows_in[...], gates[...], NN)[:slots]
-        copies[0].wait()
+        if index:
+            copies[0].wait()
         up_pre = dot(rows_in[...], ups[...], NN)[:slots]
         sigmoid = jax.nn.sigmoid(gate_pre)
         grad = act_grad[:, part]
@@ -181,7 +191,7 @@
                 value = value.T.astype(BF16)
                 for piece in range(pieces):
                     outs[piece][:, rows] = value[piece * size : (piece + 1) * size]
-        if index + depth < count:
+        if index and index + depth < count:
             for copy in reversed(fetch(index + depth)):
                 copy.start()
 
@@ -218,6 +228,10 @@
         copies[-1].start()
     for copy in copies:
         copy.wait()
+
+
+def resident(value):
+    return pltpu.with_memory_space_constraint(value, pltpu.VMEM)
 
 
 def call(body, out_shape, args, in_specs, name, limit, **kwargs):
@@ -322,25 +336,27 @@
     pieces = len(in_pieces)
     block = min(hidden, 512)
     depth = 3
-    act_grad = call(
+    first_block = pltpu.VMEM((width, block), BF16)
+    act_grad, gate_first, up_first = call(
         functools.partial(act_body, pieces=pieces, block=block),
-        shape((slots, hidden), F32),
-        (*grad_pieces, down),
-        [VMEM] * pieces + [HBM],
+        [shape((slots, hidden), F32), first_block, first_block],
+        (*grad_pieces, down, gate, up),
+        [VMEM] * pieces + [HBM] * 3,
         "act",
-        14 * MIB,
+        16 * MIB,
         scratch_shapes=[
             pltpu.VMEM((slots, width), BF16),
             pltpu.VMEM((depth, block, width), BF16),
             pltpu.SemaphoreType.DMA((depth,)),
+            pltpu.SemaphoreType.DMA((2,)),
         ],
     )
     depth = 3
     partial = call(
         functools.partial(back_body, pieces=pieces, block=block, chunk=512),
         [shape((slots // pieces, width), BF16)] * pieces,
-        (*in_pieces, act_grad, gate, up),
-        [VMEM] * (pieces + 1) + [HBM, HBM],
+        (*in_pieces, act_grad, gate, up, resident(gate_first), resident(up_first)),
+        [VMEM] * (pieces + 1) + [HBM, HBM, VMEM, VMEM],
         "back",
         40 * MIB,
         scratch_shapes=[

time: 87.6 us -> 87.5 us (level)
  transfers between devices with their start and end apart: 12 -> 12, of which waited for: 5 -> 5; matrix products, arithmetic and copies ran while one was open for 0% -> 0% of each run, Pallas kernels for 12% -> 13%
where the time goes in v4:
time: 87.5 us; the launch traced here: 87.1 us
  Pallas kernels  39.7 us (45%)
  starting transfers between devices  31.5 us (36%)
  waiting for transfers between devices  15.7 us (18%)
    pallas_call x6, Pallas kernels, call(): pl.pallas_call(body, out_shape=out_shape, in_specs=in_specs, out_specs=kw...  39.7 us
    ppermute x12, starting transfers between devices, send(): return lax.ppermute(value, AXES, pairs)  31.5 us
    ppermute x12, waiting for transfers between devices, send(): return lax.ppermute(value, AXES, pairs)  15.7 us
  transfers between devices with their start and end apart: 12, of which 5 were waited for; matrix products, arithmetic and copies ran while one was open for 0% of the time, Pallas kernels for 13%

profile of v4, /device:TPU:1, one launch (start us, length us, event | category | flops | bytes accessed | tf_op | source)
XLA Modules:
  0.0 87.1 jit_solution(13551506807071728849)
XLA Ops:
  0.0 1.9 %route.1 = (bf16[8,3072]{1,0:T(8,128)(2,1)S(1)}, bf16[8,3072]{1,0:T(8,128)(2,1)S(1)}, bf16[2,8,3072]{2,1,0:T(8,128)(2,1)S(1)}, bf16[144,3072]{1,0:T(8,128)(2,1)S(1)}) custom-call(s32[1]{0:T(128)} %bitcast.own, s32[2,128]{1,0:T(2,128)} %bitcast.20, f32[2,128]{1,0:T(2,128)} %bitcast.21, bf16[128,3072]{1,0:T(8,128)(2,1)} %bitcast.18, bf16[128,3072]{1,0:T(8,128)(2,1)} %bitcast.19), custom_call_target="tpu_custom_call" | custom-call | tf_op jit(solution)/shard_map/route/pallas_call | solution.py:244
  1.9 3.9 %collective-permute-start = (bf16[2,8,3072]{2,1,0:T(8,128)(2,1)S(1)}, bf16[2,8,3072]{2,1,0:T(8,128)(2,1)S(1)}, u32[]{:S(2)}, u32[]{:S(2)}) collective-permute-start(bf16[2,8,3072]{2,1,0:T(8,128)(2,1)S(1)} %get-tuple-element.31), channel_id=1, source_target_pairs={{8,12},{9,13},{10,14},{11,15},{12,8},{13,9},{14,10},{15,11},{16,20... | collective-permute-start | bytes 294920 | tf_op jit(solution)/shard_map/ppermute | solution.py:263
  5.8 2.0 %collective-permute-done.received = bf16[2,8,3072]{2,1,0:T(8,128)(2,1)S(1)} collective-permute-done((bf16[2,8,3072]{2,1,0:T(8,128)(2,1)S(1)}, bf16[2,8,3072]{2,1,0:T(8,128)(2,1)S(1)}, u32[]{:S(2)}, u32[]{:S(2)}) %collective-permute-start) | collective-permute-done | bytes 98336 | tf_op jit(solution)/shard_map/ppermute | solution.py:263
  7.8 1.9 %collective-permute-start.4 = (bf16[144,3072]{1,0:T(8,128)(2,1)S(1)}, bf16[144,3072]{1,0:T(8,128)(2,1)S(1)}, u32[]{:S(2)}, u32[]{:S(2)}) collective-permute-start(bf16[144,3072]{1,0:T(8,128)(2,1)S(1)} %get-tuple-element.35), channel_id=1, source_target_pairs={{8,0},{9,1},{10,2},{11,3},{12,4},{13,5},{14,6},{15,7},{16,8},{17,9... | collective-permute-start | bytes 2654216 | tf_op jit(solution)/shard_map/ppermute | solution.py:263
  9.8 3.4 %collective-permute-start.3 = (bf16[2,16,3072]{2,1,0:T(8,128)(2,1)S(1)}, bf16[2,16,3072]{2,1,0:T(8,128)(2,1)S(1)}, u32[]{:S(2)}, u32[]{:S(2)}) collective-permute-start(bf16[2,16,3072]{2,1,0:T(8,128)(2,1)S(1)} %get-tuple-element.34), channel_id=1, source_target_pairs={{8,9},{9,8},{10,11},{11,10},{12,13},{13,12},{14,15},{15,14},{16,17... | collective-permute-start | bytes 589832 | tf_op jit(solution)/shard_map/ppermute | solution.py:263
  13.3 4.2 %collective-permute-start.2 = (bf16[16,3072]{1,0:T(8,128)(2,1)S(1)}, bf16[16,3072]{1,0:T(8,128)(2,1)S(1)}, u32[]{:S(2)}, u32[]{:S(2)}) collective-permute-start(bf16[16,3072]{1,0:T(8,128)(2,1)S(1)} %get-tuple-element.41.refs_3_), channel_id=1, source_target_pairs={{8,10},{9,11},{10,8},{11,9},{12,14},{13,15},{14,12},{15,13},{16,18... | collective-permute-start | bytes 294920 | tf_op jit(solution)/shard_map/ppermute | solution.py:263
  17.5 1.9 %collective-permute-start.1 = (bf16[16,3072]{1,0:T(8,128)(2,1)S(1)}, bf16[16,3072]{1,0:T(8,128)(2,1)S(1)}, u32[]{:S(2)}, u32[]{:S(2)}) collective-permute-start(bf16[16,3072]{1,0:T(8,128)(2,1)S(1)} %get-tuple-element.41.refs_3_), channel_id=1, source_target_pairs={{8,11},{9,10},{10,9},{11,8},{12,15},{13,14},{14,13},{15,12},{16,19... | collective-permute-start | bytes 294920 | tf_op jit(solution)/shard_map/ppermute | solution.py:263
  19.4 3.2 %collective-permute-start.6 = (bf16[16,3072]{1,0:T(8,128)(2,1)S(1)}, bf16[16,3072]{1,0:T(8,128)(2,1)S(1)}, u32[]{:S(2)}, u32[]{:S(2)}) collective-permute-start(bf16[16,3072]{1,0:T(8,128)(2,1)S(1)} %get-tuple-element.37.refs_3_), channel_id=1, source_target_pairs={{8,10},{9,11},{10,8},{11,9},{12,14},{13,15},{14,12},{15,13},{16,18... | collective-permute-start | bytes 294920 | tf_op jit(solution)/shard_map/ppermute | solution.py:263
  22.7 0.0 collective-permute-done.2.refs_1_
  22.7 3.8 %collective-permute-start.5 = (bf16[16,3072]{1,0:T(8,128)(2,1)S(1)}, bf16[16,3072]{1,0:T(8,128)(2,1)S(1)}, u32[]{:S(2)}, u32[]{:S(2)}) collective-permute-start(bf16[16,3072]{1,0:T(8,128)(2,1)S(1)} %get-tuple-element.37.refs_3_), channel_id=1, source_target_pairs={{8,11},{9,10},{10,9},{11,8},{12,15},{13,14},{14,13},{15,12},{16,19... | collective-permute-start | bytes 294920 | tf_op jit(solution)/shard_map/ppermute | solution.py:263
  26.5 0.0 collective-permute-done.1.refs_0_
  26.5 0.0 collective-permute-done.3.refs_2_
  26.6 11.1 %act.1 = (f32[64,4096]{1,0:T(8,128)S(1)}, bf16[3072,512]{1,0:T(8,128)(2,1)S(1)}, bf16[3072,512]{1,0:T(8,128)(2,1)S(1)}) custom-call(bf16[16,3072]{1,0:T(8,128)(2,1)S(1)} %collective-permute-done.1.refs_0_, bf16[16,3072]{1,0:T(8,128)(2,1)S(1)} %collective-permute-done.2.refs_1_, bf16[2,16,3072]{2,1,0:T(8,128)(2,1)S(1)} %collective-permute-done.3.refs_2_, ...), custom_call_target="tpu_custom_call" | custom-call | tf_op jit(solution)/shard_map/act/pallas_call | solution.py:244
  37.7 24.5 %back.1 = (bf16[16,3072]{1,0:T(8,128)(2,1)S(1)}, bf16[16,3072]{1,0:T(8,128)(2,1)S(1)}, bf16[16,3072]{1,0:T(8,128)(2,1)S(1)}, bf16[16,3072]{1,0:T(8,128)(2,1)S(1)}) custom-call(bf16[16,3072]{1,0:T(8,128)(2,1)S(1)} %collective-permute-done.5.refs_0_, bf16[16,3072]{1,0:T(8,128)(2,1)S(1)} %collective-permute-done.6.refs_1_, ...), custom_call_target="tpu_custom_call" | custom-call | tf_op jit(solution)/shard_map/back/pallas_call | solution.py:244
  62.1 1.9 %collective-permute-start.7 = (bf16[16,3072]{1,0:T(8,128)(2,1)S(1)}, bf16[16,3072]{1,0:T(8,128)(2,1)S(1)}, u32[]{:S(2)}, u32[]{:S(2)}) collective-permute-start(bf16[16,3072]{1,0:T(8,128)(2,1)S(1)} %get-tuple-element.45), channel_id=1, source_target_pairs={{8,3},{9,2},{10,1},{11,0},{12,7},{13,6},{14,5},{15,4},{16,11},{17,... | collective-permute-start | bytes 294920 | tf_op jit(solution)/shard_map/ppermute | solution.py:263
  64.1 1.9 %collective-permute-start.8 = (bf16[16,3072]{1,0:T(8,128)(2,1)S(1)}, bf16[16,3072]{1,0:T(8,128)(2,1)S(1)}, u32[]{:S(2)}, u32[]{:S(2)}) collective-permute-start(bf16[16,3072]{1,0:T(8,128)(2,1)S(1)} %get-tuple-element.46), channel_id=1, source_target_pairs={{8,2},{9,3},{10,0},{11,1},{12,6},{13,7},{14,4},{15,5},{16,10},{17,... | collective-permute-start | bytes 294920 | tf_op jit(solution)/shard_map/ppermute | solution.py:263
  66.0 1.9 %collective-permute-start.9 = (bf16[16,3072]{1,0:T(8,128)(2,1)S(1)}, bf16[16,3072]{1,0:T(8,128)(2,1)S(1)}, u32[]{:S(2)}, u32[]{:S(2)}) collective-permute-start(bf16[16,3072]{1,0:T(8,128)(2,1)S(1)} %get-tuple-element.47), channel_id=1, source_target_pairs={{8,1},{9,0},{10,3},{11,2},{12,5},{13,4},{14,7},{15,6},{16,9},{17,8... | collective-permute-start | bytes 294920 | tf_op jit(solution)/shard_map/ppermute | solution.py:263
  67.9 1.9 %collective-permute-start.10 = (bf16[16,3072]{1,0:T(8,128)(2,1)S(1)}, bf16[16,3072]{1,0:T(8,128)(2,1)S(1)}, u32[]{:S(2)}, u32[]{:S(2)}) collective-permute-start(bf16[16,3072]{1,0:T(8,128)(2,1)S(1)} %get-tuple-element.48), channel_id=1, source_target_pairs={{8,0},{9,1},{10,2},{11,3},{12,4},{13,5},{14,6},{15,7},{16,8},{17,9... | collective-permute-start | bytes 294920 | tf_op jit(solution)/shard_map/ppermute | solution.py:263
  69.8 5.2 %collective-permute-done.7.refs_0_ = bf16[16,3072]{1,0:T(8,128)(2,1)S(1)} collective-permute-done((bf16[16,3072]{1,0:T(8,128)(2,1)S(1)}, bf16[16,3072]{1,0:T(8,128)(2,1)S(1)}, u32[]{:S(2)}, u32[]{:S(2)}) %collective-permute-start.7) | collective-permute-done | bytes 98336 | tf_op jit(solution)/shard_map/ppermute | solution.py:263
  75.0 4.4 %collective-permute-done.8.refs_1_ = bf16[16,3072]{1,0:T(8,128)(2,1)S(1)} collective-permute-done((bf16[16,3072]{1,0:T(8,128)(2,1)S(1)}, bf16[16,3072]{1,0:T(8,128)(2,1)S(1)}, u32[]{:S(2)}, u32[]{:S(2)}) %collective-permute-start.8) | collective-permute-done | bytes 98336 | tf_op jit(solution)/shard_map/ppermute | solution.py:263
  79.4 1.9 %collective-permute-done.10.refs_3_ = bf16[16,3072]{1,0:T(8,128)(2,1)S(1)} collective-permute-done((bf16[16,3072]{1,0:T(8,128)(2,1)S(1)}, bf16[16,3072]{1,0:T(8,128)(2,1)S(1)}, u32[]{:S(2)}, u32[]{:S(2)}) %collective-permute-start.10) | collective-permute-done | bytes 98336 | tf_op jit(solution)/shard_map/ppermute | solution.py:263
  81.3 1.3 %collective-permute-start.11 = (f32[8,3072]{1,0:T(8,128)S(1)}, f32[8,3072]{1,0:T(8,128)S(1)}, u32[]{:S(2)}, u32[]{:S(2)}) collective-permute-start(f32[8,3072]{1,0:T(8,128)S(1)} %get-tuple-element.50), channel_id=1, source_target_pairs={{0,4},{1,5},{2,6},{3,7},{4,0},{5,1},{6,2},{7,3},{8,12},{9,13},{10,... | collective-permute-start | bytes 294920 | tf_op jit(solution)/shard_map/ppermute | solution.py:263
  82.6 2.3 %collective-permute-done.11.received = f32[8,3072]{1,0:T(8,128)S(1)} collective-permute-done((f32[8,3072]{1,0:T(8,128)S(1)}, f32[8,3072]{1,0:T(8,128)S(1)}, u32[]{:S(2)}, u32[]{:S(2)}) %collective-permute-start.11) | collective-permute-done | bytes 98336 | tf_op jit(solution)/shard_map/ppermute | solution.py:263
  84.8 2.1 %place.1 = bf16[128,3072]{1,0:T(8,128)(2,1)} custom-call(bf16[144,3072]{1,0:T(8,128)(2,1)S(1)} %collective-permute-done.4.ahead, f32[8,3072]{1,0:T(8,128)S(1)} %get-tuple-element.49.kept, f32[8,3072]{1,0:T(8,128)S(1)} %collective-permute-done.11.received), custom_call_target="tpu_custom_call" | custom-call | tf_op jit(solution)/shard_map/place/pallas_call | solution.py:244
  (6 shorter events, 0.1 us)
Async XLA Ops:
  1.9 5.9 %collective-permute-start = (bf16[2,8,3072]{2,1,0:T(8,128)(2,1)S(1)}, bf16[2,8,3072]{2,1,0:T(8,128)(2,1)S(1)}, u32[]{:S(2)}, u32[]{:S(2)}) collective-permute-start(bf16[2,8,3072]{2,1,0:T(8,128)(2,1)S(1)} %get-tuple-element.31), channel_id=1, source_target_pairs={{8,12},{9,13},{10,14},{11,15},{12,8},{13,9},{14,10},{15,11},{16,20... | collective-permute-start | bytes 294920 | tf_op jit(solution)/shard_map/ppermute | solution.py:263
  7.8 18.7 %collective-permute-start.4 = (bf16[144,3072]{1,0:T(8,128)(2,1)S(1)}, bf16[144,3072]{1,0:T(8,128)(2,1)S(1)}, u32[]{:S(2)}, u32[]{:S(2)}) collective-permute-start(bf16[144,3072]{1,0:T(8,128)(2,1)S(1)} %get-tuple-element.35), channel_id=1, source_target_pairs={{8,0},{9,1},{10,2},{11,3},{12,4},{13,5},{14,6},{15,7},{16,8},{17,9... | collective-permute-start | bytes 2654216 | tf_op jit(solution)/shard_map/ppermute | solution.py:263
  9.8 16.7 %collective-permute-start.3 = (bf16[2,16,3072]{2,1,0:T(8,128)(2,1)S(1)}, bf16[2,16,3072]{2,1,0:T(8,128)(2,1)S(1)}, u32[]{:S(2)}, u32[]{:S(2)}) collective-permute-start(bf16[2,16,3072]{2,1,0:T(8,128)(2,1)S(1)} %get-tuple-element.34), channel_id=1, source_target_pairs={{8,9},{9,8},{10,11},{11,10},{12,13},{13,12},{14,15},{15,14},{16,17... | collective-permute-start | bytes 589832 | tf_op jit(solution)/shard_map/ppermute | solution.py:263
  13.3 9.4 %collective-permute-start.2 = (bf16[16,3072]{1,0:T(8,128)(2,1)S(1)}, bf16[16,3072]{1,0:T(8,128)(2,1)S(1)}, u32[]{:S(2)}, u32[]{:S(2)}) collective-permute-start(bf16[16,3072]{1,0:T(8,128)(2,1)S(1)} %get-tuple-element.41.refs_3_), channel_id=1, source_target_pairs={{8,10},{9,11},{10,8},{11,9},{12,14},{13,15},{14,12},{15,13},{16,18... | collective-permute-start | bytes 294920 | tf_op jit(solution)/shard_map/ppermute | solution.py:263
  17.5 9.0 %collective-permute-start.1 = (bf16[16,3072]{1,0:T(8,128)(2,1)S(1)}, bf16[16,3072]{1,0:T(8,128)(2,1)S(1)}, u32[]{:S(2)}, u32[]{:S(2)}) collective-permute-start(bf16[16,3072]{1,0:T(8,128)(2,1)S(1)} %get-tuple-element.41.refs_3_), channel_id=1, source_target_pairs={{8,11},{9,10},{10,9},{11,8},{12,15},{13,14},{14,13},{15,12},{16,19... | collective-permute-start | bytes 294920 | tf_op jit(solution)/shard_map/ppermute | solution.py:263
  19.4 18.2 %collective-permute-start.6 = (bf16[16,3072]{1,0:T(8,128)(2,1)S(1)}, bf16[16,3072]{1,0:T(8,128)(2,1)S(1)}, u32[]{:S(2)}, u32[]{:S(2)}) collective-permute-start(bf16[16,3072]{1,0:T(8,128)(2,1)S(1)} %get-tuple-element.37.refs_3_), channel_id=1, source_target_pairs={{8,10},{9,11},{10,8},{11,9},{12,14},{13,15},{14,12},{15,13},{16,18... | collective-permute-start | bytes 294920 | tf_op jit(solution)/shard_map/ppermute | solution.py:263
  22.7 15.0 %collective-permute-start.5 = (bf16[16,3072]{1,0:T(8,128)(2,1)S(1)}, bf16[16,3072]{1,0:T(8,128)(2,1)S(1)}, u32[]{:S(2)}, u32[]{:S(2)}) collective-permute-start(bf16[16,3072]{1,0:T(8,128)(2,1)S(1)} %get-tuple-element.37.refs_3_), channel_id=1, source_target_pairs={{8,11},{9,10},{10,9},{11,8},{12,15},{13,14},{14,13},{15,12},{16,19... | collective-permute-start | bytes 294920 | tf_op jit(solution)/shard_map/ppermute | solution.py:263
  62.1 12.9 %collective-permute-start.7 = (bf16[16,3072]{1,0:T(8,128)(2,1)S(1)}, bf16[16,3072]{1,0:T(8,128)(2,1)S(1)}, u32[]{:S(2)}, u32[]{:S(2)}) collective-permute-start(bf16[16,3072]{1,0:T(8,128)(2,1)S(1)} %get-tuple-element.45), channel_id=1, source_target_pairs={{8,3},{9,2},{10,1},{11,0},{12,7},{13,6},{14,5},{15,4},{16,11},{17,... | collective-permute-start | bytes 294920 | tf_op jit(solution)/shard_map/ppermute | solution.py:263
  64.1 15.3 %collective-permute-start.8 = (bf16[16,3072]{1,0:T(8,128)(2,1)S(1)}, bf16[16,3072]{1,0:T(8,128)(2,1)S(1)}, u32[]{:S(2)}, u32[]{:S(2)}) collective-permute-start(bf16[16,3072]{1,0:T(8,128)(2,1)S(1)} %get-tuple-element.46), channel_id=1, source_target_pairs={{8,2},{9,3},{10,0},{11,1},{12,6},{13,7},{14,4},{15,5},{16,10},{17,... | collective-permute-start | bytes 294920 | tf_op jit(solution)/shard_map/ppermute | solution.py:263
  66.0 13.4 %collective-permute-start.9 = (bf16[16,3072]{1,0:T(8,128)(2,1)S(1)}, bf16[16,3072]{1,0:T(8,128)(2,1)S(1)}, u32[]{:S(2)}, u32[]{:S(2)}) collective-permute-start(bf16[16,3072]{1,0:T(8,128)(2,1)S(1)} %get-tuple-element.47), channel_id=1, source_target_pairs={{8,1},{9,0},{10,3},{11,2},{12,5},{13,4},{14,7},{15,6},{16,9},{17,8... | collective-permute-start | bytes 294920 | tf_op jit(solution)/shard_map/ppermute | solution.py:263
  67.9 13.3 %collective-permute-start.10 = (bf16[16,3072]{1,0:T(8,128)(2,1)S(1)}, bf16[16,3072]{1,0:T(8,128)(2,1)S(1)}, u32[]{:S(2)}, u32[]{:S(2)}) collective-permute-start(bf16[16,3072]{1,0:T(8,128)(2,1)S(1)} %get-tuple-element.48), channel_id=1, source_target_pairs={{8,0},{9,1},{10,2},{11,3},{12,4},{13,5},{14,6},{15,7},{16,8},{17,9... | collective-permute-start | bytes 294920 | tf_op jit(solution)/shard_map/ppermute | solution.py:263
  81.3 3.5 %collective-permute-start.11 = (f32[8,3072]{1,0:T(8,128)S(1)}, f32[8,3072]{1,0:T(8,128)S(1)}, u32[]{:S(2)}, u32[]{:S(2)}) collective-permute-start(f32[8,3072]{1,0:T(8,128)S(1)} %get-tuple-element.50), channel_id=1, source_target_pairs={{0,4},{1,5},{2,6},{3,7},{4,0},{5,1},{6,2},{7,3},{8,12},{9,13},{10,... | collective-permute-start | bytes 294920 | tf_op jit(solution)/shard_map/ppermute | solution.py:263
